TPU v7x, 256 devices: a whole 4x4x8 slice. The times are simulated.
256 devices in a mesh: grp: 32 (over z, y), tp: 8 (over x, core).
Axes of the slice: x: 4, y: 4, z: 8, core: 2. Of those that a mesh axis runs over, the one named last changes fastest.
Arguments:
- hidden: bfloat16 [24576, 4608], P('grp', 'tp'), as said below
- norm_gain: float32 [4608], replicated, may hold values from 0.1 to 1.9
- q_weight: bfloat16 [4608, 2048], P(None, 'tp'), as said below
- k_weight: bfloat16 [4608, 1024], P(None, 'tp'), as said below
- v_weight: bfloat16 [4608, 1024], P(None, 'tp'), may hold values from -0.09375 to 0.09375
- kv_pages: bfloat16 [16384, 16, 8, 256], P('grp', None, 'tp'), as said below
- page_table: int32 [512, 256], P('grp'), may hold values from 0 to 575
- cache_len: int32 [512], P('grp'), may hold values from 1 to 4096, as said below
- tree_parent: int32 [512, 48], P('grp'), may hold values from -1 to 46, as said below
- accept_node: int32 [512], P('grp'), may hold values from 0 to 47
- pair_slot: int32 [32, 2], P('grp'), may hold values from 0 to 15, as said below
- far_len: int32 [32, 2], replicated, may hold values from 1 to 4096, as said below
- far_table: int32 [64, 256], P('grp'), may hold values from 0 to 575
- mig_src: int32 [2048], P('grp'), may hold values from 0 to 31, as said below
- mig_page: int32 [2048], P('grp'), may hold values from 0 to 511
Outputs:
- attn_out: bfloat16 [24576, 2048], P('grp', 'tp')
- accepted: bfloat16 [2560, 8, 256], P('grp', 'tp')
Inputs may be any that keep to these rules, and one draw needn't show every extreme that they name: `hidden`: entries within 4 times a scale of order one, with column scales spread over a factor of ten. `q_weight`: entries within 4 / sqrt(4608). `k_weight`: entries within 9 / sqrt(4608). `kv_pages`: finite, of order one, some key entries larger. `cache_len`: some request has exactly 4096 cached tokens. `tree_parent`: node 0 is the root with parent -1; nodes are ordered by depth and each parent is an earlier node one level up; depths are at most 4 and every tree has a node of depth 4. `pair_slot`: the 2 slots of a group differ. `far_len`: some entry is exactly 4096. `mig_src`: never the receiving group itself; at most 4 of a group's entries name one source, and in every group exactly 4 name one source.
All inputs are finite; a program needn't handle non-finite values.
Results may differ from a plain program's by a relative error of at most 0.012.
Values may be sent and summed in bfloat16 or wider, within the bound.
A program may use at most 128 MiB of HBM per device.

v0:
```python
import jax
import jax.numpy as jnp
from jax import lax
from jax.sharding import PartitionSpec as P

D = 4608
CAP = 4
ACCEPT = 5


THETA_LOG = 9.210340371976184
SCORE_SCALE = 144.0 ** (-0.5)
LOGIT_CAP = 50.0
HIGHEST = lax.Precision.HIGHEST


def partner(value, axis, bit):
    mask = 2**bit
    pairs = [(source, source ^ mask) for source in range(lax.axis_size(axis))]
    return lax.ppermute(value, axis, pairs)


def rotate(values, position):
    halfway = values.shape[-1] // 2
    angles = jnp.exp(-THETA_LOG * 2.0 * jnp.arange(halfway, dtype=jnp.float32) / values.shape[-1])
    phases = position.astype(jnp.float32)[:, None] * angles[None, :]
    cosine = jnp.cos(phases)[:, None, :]
    sine_part = jnp.sin(phases)[:, None, :]
    former = values[..., :halfway]
    latter = values[..., halfway:]
    return jnp.concatenate(
        [former * cosine - latter * sine_part, latter * cosine + former * sine_part], -1
    )


def ancestry(parents):
    length = parents.shape[-1]
    labels = jnp.arange(length, dtype=jnp.int32)
    reached = (parents[..., :, None] == labels).astype(jnp.float32) + jnp.eye(
        length, dtype=jnp.float32
    )
    reached = jnp.minimum(jnp.einsum("nij,njk->nik", reached, reached, precision=HIGHEST), 1.0)
    reached = jnp.minimum(jnp.einsum("nij,njk->nik", reached, reached, precision=HIGHEST), 1.0)
    depths = jnp.sum((reached > 0.5).astype(jnp.int32), -1) - 1
    return (reached, depths)


def absorb(running, queries, keys_block, values_block, allowed):
    largest, summed, weighted = running
    scores = (
        jnp.einsum("igrd,tgd->igrt", queries, keys_block, preferred_element_type=jnp.float32)
        * SCORE_SCALE
    )
    scores = LOGIT_CAP * jnp.tanh(scores / LOGIT_CAP)
    weights = jnp.where(allowed, jnp.exp(scores - LOGIT_CAP), 0.0)
    summed = summed + jnp.sum(weights, -1)
    weighted = weighted + jnp.einsum(
        "igrt,tgd->igrd",
        weights.astype(jnp.bfloat16),
        values_block,
        preferred_element_type=jnp.float32,
    )
    return (largest, summed, weighted)


def empty_state(queries):
    leading = queries.shape[:3]
    return (
        jnp.full(leading, LOGIT_CAP, jnp.float32),
        jnp.zeros(leading, jnp.float32),
        jnp.zeros(queries.shape, jnp.float32),
    )


def attend_blocks(queries, loader, length, block_span):
    turns = (length + block_span - 1) // block_span

    def advance(number, running):
        keys_block, values_block = loader(number)
        allowed = (number * block_span + jnp.arange(block_span, dtype=jnp.int32) < length)[
            None, None, None, :
        ]
        return absorb(running, queries, keys_block, values_block, allowed)

    return lax.fori_loop(0, turns, advance, empty_state(queries))


def combine(states):
    summed = jnp.zeros(states[0][1].shape, jnp.float32)
    weighted = jnp.zeros(states[0][2].shape, jnp.float32)
    for state in states:
        summed = summed + state[1]
        weighted = weighted + state[2]
    return weighted / summed[..., None]


def body(
    hidden,
    norm_gain,
    q_weight,
    k_weight,
    v_weight,
    kv_pages,
    page_table,
    cache_len,
    tree_parent,
    accept_node,
    pair_slot,
    far_len,
    far_table,
    mig_src,
    mig_page,
):
    token_rows = hidden.shape[0]
    requests = cache_len.shape[0]
    tree_size = tree_parent.shape[1]
    head_size = kv_pages.shape[3] // 2
    local_heads = kv_pages.shape[2]
    page_size = kv_pages.shape[1]
    table_width = page_table.shape[1]
    long_count = pair_slot.shape[1]
    migrations = mig_src.shape[0]
    groups = lax.axis_size("grp")
    myself = lax.axis_index("grp")
    widened = lax.all_gather(hidden, "tp", axis=1, tiled=True).astype(jnp.float32)
    scaled = (widened * norm_gain[None, :]).astype(jnp.bfloat16)
    query_sum = jnp.dot(scaled, q_weight, preferred_element_type=jnp.float32)
    key_sum = jnp.dot(scaled, k_weight, preferred_element_type=jnp.float32)
    value_sum = jnp.dot(scaled, v_weight, preferred_element_type=jnp.float32)
    squares = jnp.sum(widened * widened, 1)
    query_sum, key_sum, value_sum, squares = (query_sum, key_sum, value_sum, squares)
    row_scale = lax.rsqrt(squares / D + 1e-06)[:, None]
    reached, depths = ancestry(tree_parent)
    far_mine = lax.dynamic_index_in_dim(far_len, myself, 0, keepdims=False)
    long_slots = pair_slot[0]
    matched = jnp.arange(requests, dtype=jnp.int32)[:, None] == long_slots[None, :]
    far_own = jnp.sum(jnp.where(matched, far_mine[None, :], 0), 1)
    position = ((cache_len + far_own)[:, None] + depths).reshape(-1)
    queries = rotate(
        (query_sum * row_scale).reshape(token_rows, 2 * local_heads, head_size), position
    ).astype(jnp.bfloat16)
    keys_new = rotate(
        (key_sum * row_scale).reshape(token_rows, local_heads, head_size), position
    ).astype(jnp.bfloat16)
    values_new = (
        (value_sum * row_scale).astype(jnp.bfloat16).reshape(token_rows, local_heads, head_size)
    )
    order_index = jnp.arange(migrations, dtype=jnp.int32)
    earlier = order_index[:, None] > order_index[None, :]

    def rank_of(sources):
        return jnp.sum(
            ((sources[..., :, None] == sources[..., None, :]) & earlier).astype(jnp.int32), -1
        )

    own_rank = rank_of(mig_src)
    slot_index = jnp.arange(CAP, dtype=jnp.int32)
    every_source, every_page = (
        lax.all_gather(mig_src, "grp", axis=0, tiled=True),
        lax.all_gather(mig_page, "grp", axis=0, tiled=True),
    )
    every_source = every_source.reshape(groups, migrations)
    every_page = every_page.reshape(groups, migrations)
    every_rank = rank_of(every_source)
    hits = (every_source[:, :, None] == myself) & (
        every_rank[:, :, None] == slot_index[None, None, :]
    )
    wanted = jnp.sum(jnp.where(hits, every_page[:, :, None] + 1, 0), 1) - 1
    present = (wanted >= 0)[:, :, None, None, None]
    outgoing = jnp.where(present, kv_pages[jnp.maximum(wanted, 0)], jnp.zeros((), jnp.bfloat16))
    incoming = lax.all_to_all(outgoing, "grp", split_axis=0, concat_axis=0, tiled=True)
    moved = incoming.reshape(groups * CAP, page_size, local_heads, 2 * head_size)[
        mig_src * CAP + own_rank
    ]
    extended = jnp.concatenate([kv_pages, moved], 0)
    block_pages = min(32, table_width)
    block_span = block_pages * page_size

    def page_loader(table_row):

        def loader(number):
            chosen = lax.dynamic_slice_in_dim(table_row, number * block_pages, block_pages, 0)
            gathered = extended[chosen].reshape(block_span, local_heads, 2 * head_size)
            return (gathered[..., :head_size], gathered[..., head_size:])

        return loader

    grouped = queries.reshape(requests, tree_size, local_heads, 2, head_size)
    long_queries = grouped[long_slots]
    far_dense = extended[far_table].reshape(
        long_count, table_width * page_size, local_heads, 2 * head_size
    )
    arrived = partner(far_dense, "grp", 0)

    def owner_part(packed):
        query_block, cache_block, length = packed

        def loader(number):
            portion = lax.dynamic_slice_in_dim(cache_block, number * block_span, block_span, 0)
            return (portion[..., :head_size], portion[..., head_size:])

        return attend_blocks(query_block, loader, length, block_span)

    far_parts = lax.map(owner_part, (long_queries, arrived, far_mine))
    keys_grouped = keys_new.reshape(requests, tree_size, local_heads, head_size)
    values_grouped = values_new.reshape(requests, tree_size, local_heads, head_size)

    def request_part(packed):
        query_block, key_block, value_block, table_row, length, tree_mask, match_row = packed
        own_state = attend_blocks(query_block, page_loader(table_row), length, block_span)
        tree_state = absorb(
            empty_state(query_block),
            query_block,
            key_block,
            value_block,
            (tree_mask > 0.5)[:, None, None, :],
        )
        chooser = match_row[:, None, None, None]
        far_state = (
            own_state[0],
            jnp.sum(jnp.where(chooser, far_parts[1], 0.0), 0),
            jnp.sum(jnp.where(match_row[:, None, None, None, None], far_parts[2], 0.0), 0),
        )
        mixed = combine((own_state, tree_state, far_state))
        return mixed.reshape(tree_size, 2 * local_heads * head_size).astype(jnp.bfloat16)

    attn_out = lax.map(
        request_part,
        (grouped, keys_grouped, values_grouped, page_table, cache_len, reached, matched),
    ).reshape(token_rows, 2 * local_heads * head_size)
    leaves = (jnp.arange(tree_size, dtype=jnp.int32)[None, :] == accept_node[:, None]).astype(
        jnp.float32
    )
    lineage = jnp.einsum("rt,rtj->rj", leaves, reached, precision=HIGHEST)
    levels = (depths[:, None, :] == jnp.arange(ACCEPT, dtype=jnp.int32)[None, :, None]).astype(
        jnp.float32
    )
    picker = lineage[:, None, :] * levels
    fresh_rows = (
        jnp.concatenate([keys_new, values_new], -1)
        .reshape(requests, tree_size, local_heads * 2 * head_size)
        .astype(jnp.float32)
    )
    accepted = (
        jnp.einsum("rpt,rtc->rpc", picker, fresh_rows, precision=HIGHEST)
        .astype(jnp.bfloat16)
        .reshape(requests * ACCEPT, local_heads, 2 * head_size)
    )
    return (attn_out, accepted)


def solution(mesh):
    in_specs = (
        P("grp", "tp"),
        P(),
        P(None, "tp"),
        P(None, "tp"),
        P(None, "tp"),
        P("grp", None, "tp", None),
        P("grp", None),
        P("grp"),
        P("grp", None),
        P("grp"),
        P("grp", None),
        P(),
        P("grp", None),
        P("grp"),
        P("grp"),
    )
    out_specs = (P("grp", "tp"), P("grp", "tp", None))
    return jax.shard_map(body, mesh=mesh, in_specs=in_specs, out_specs=out_specs, check_vma=False)
```

profile of v0, /device:TPU:132, one launch (start us, length us, event | category | flops | bytes accessed | tf_op | source)
XLA Modules:
  0.0 746.0 jit_solution(10805936506623166716)
XLA Ops:
  11.6 141.3 %all-reduce.2 = (s32[2048]{0:T(1024)S(1)}, s32[2048]{0:T(1024)S(1)}) all-reduce(s32[2048]{0:T(1024)S(1)} %dynamic-update-slice.1, s32[2048]{0:T(1024)S(1)} %dynamic-update-slice), channel_id=1, replica_groups=mesh['grp'=32,'tp'=8] {'grp'}, use_global_device_ids=true, to_apply=%add.1 | all-reduce | flops 4096 | bytes 32768
  158.7 9.9 %all-to-all-start = ((bf16[32,4,16,1,256]{4,2,1,3,0:T(8,128)(2,1)}), bf16[32,4,16,1,256]{4,2,1,3,0:T(8,128)(2,1)}, u32[]{:S(2)}, u32[]{:S(2)}) async-start(bf16[32,4,16,1,256]{4,2,1,3,0:T(8,128)(2,1)} %broadcast_select_fusion), calls=%async_computation | async-start | bytes 2097152 | tf_op jit(solution)/shard_map/all_to_all | solution.py:171
  171.2 12.9 %all-to-all-done = bf16[32,4,16,1,256]{4,2,1,3,0:T(8,128)(2,1)} async-done(((bf16[32,4,16,1,256]{4,2,1,3,0:T(8,128)(2,1)}), bf16[32,4,16,1,256]{4,2,1,3,0:T(8,128)(2,1)}, u32[]{:S(2)}, u32[]{:S(2)}) %all-to-all-start) | async-done | bytes 1048608 | tf_op jit(solution)/shard_map/all_to_all | solution.py:171
  186.7 6.5 fusion.85
  193.2 5.3 gather_fusion.3
  200.0 4.6 fusion.46
  205.0 4.4 fusion.47
  211.4 3.0 fusion.48
  216.1 5.3 convolution_multiply_fusion.3
  235.3 30.2 %collective-permute-done = bf16[2,4096,1,256]{3,1,2,0:T(8,128)(2,1)} collective-permute-done((bf16[2,4096,1,256]{3,1,2,0:T(8,128)(2,1)}, bf16[2,4096,1,256]{3,1,2,0:T(8,128)(2,1)}, u32[]{:S(2)}, u32[]{:S(2)}) %collective-permute-start) | collective-permute-done | bytes 4194336 | tf_op jit(solution)/shard_map/ppermute | solution.py:20
  265.4 54.3 %while.103 = (s32[]{:T(128)}, f32[2,48,1,2]{1,3,2,0:T(2,128)S(1)}, f32[2,48,1,2,128]{4,3,2,1,0:T(2,128)S(1)}, s32[2]{0:T(128)S(1)}, bf16[2,4096,1,256]{3,1,2,0:T...) while((s32[]{:T(128)}, f32[2,48,1,2]{1,3,2,0:T(2,128)S(1)}, ...), condition=%wide.region_10.11_spmd, body=%wide.region_6.10_spmd.sunk | while | flops 25474072 | bytes 4978198 | solution.py:204
  266.8 3.1 dynamic-slice_bitcast_fusion.13
  269.9 21.1 %while.106 = (s32[]{:T(128)}, f32[48,1,2]{0,2,1:T(2,128)S(1)}, f32[48,1,2,128]{3,0,2,1:T(8,128)S(1)}, s32[]{:T(128)}, s32[]{:T(128)}, /*index=5*/bf16[4096,1,256...) while((s32[]{:T(128)}, f32[48,1,2]{0,2,1:T(2,128)S(1)}, ...), condition=%wide.region_9.9_spmd, body=%wide.region_7.8_spmd.sunk | while | flops 25474056 | bytes 584387 | solution.py:85
  292.4 3.1 dynamic-slice_bitcast_fusion.13
  295.5 24.1 %while.106 = (s32[]{:T(128)}, f32[48,1,2]{0,2,1:T(2,128)S(1)}, f32[48,1,2,128]{3,0,2,1:T(8,128)S(1)}, s32[]{:T(128)}, s32[]{:T(128)}, /*index=5*/bf16[4096,1,256...) while((s32[]{:T(128)}, f32[48,1,2]{0,2,1:T(2,128)S(1)}, ...), condition=%wide.region_9.9_spmd, body=%wide.region_7.8_spmd.sunk | while | flops 25474056 | bytes 584387 | solution.py:85
  320.5 418.7 %while.105 = (s32[]{:T(128)}, bf16[16,48,256]{2,1,0:T(8,128)(2,1)}, s32[16]{0:T(128)S(1)}, s32[16,256]{1,0:T(8,128)}, bf16[16,48,1,2,128]{4,1,3,2,0:T(8,128)(2,1...) while((s32[]{:T(128)}, bf16[16,48,256]{2,1,0:T(8,128)(2,1)}, ...), condition=%wide.region_18.19_spmd, body=%wide.region_11.18_spmd.sunk | while | flops 27950840 | bytes 1755110 | solution.py:227
  324.6 8.3 %while.107 = (s32[]{:T(128)}, f32[48,1,2]{0,2,1:T(2,128)S(1)}, f32[48,1,2,128]{3,0,2,1:T(8,128)S(1)}, s32[]{:T(128)}, s32[]{:T(128)}, /*index=5*/s32[256]{0:T(25...) while((s32[]{:T(128)}, f32[48,1,2]{0,2,1:T(2,128)S(1)}, ...), condition=%wide.region_14.14_spmd, body=%wide.region_12.13_spmd.sunk | while | flops 25475176 | bytes 1113291 | solution.py:85
  325.3 2.9 gather_fusion
  329.5 2.9 gather_fusion
  338.5 29.1 %while.107 = (s32[]{:T(128)}, f32[48,1,2]{0,2,1:T(2,128)S(1)}, f32[48,1,2,128]{3,0,2,1:T(8,128)S(1)}, s32[]{:T(128)}, s32[]{:T(128)}, /*index=5*/s32[256]{0:T(25...) while((s32[]{:T(128)}, f32[48,1,2]{0,2,1:T(2,128)S(1)}, ...), condition=%wide.region_14.14_spmd, body=%wide.region_12.13_spmd.sunk | while | flops 25475176 | bytes 1113291 | solution.py:85
  339.3 2.9 gather_fusion
  343.4 2.9 gather_fusion
  347.6 2.9 gather_fusion
  351.7 2.9 gather_fusion
  355.9 2.9 gather_fusion
  360.0 2.9 gather_fusion
  364.2 2.9 gather_fusion
  373.3 4.2 while.107
  374.0 2.9 gather_fusion
  383.1 16.6 %while.107 = (s32[]{:T(128)}, f32[48,1,2]{0,2,1:T(2,128)S(1)}, f32[48,1,2,128]{3,0,2,1:T(8,128)S(1)}, s32[]{:T(128)}, s32[]{:T(128)}, /*index=5*/s32[256]{0:T(25...) while((s32[]{:T(128)}, f32[48,1,2]{0,2,1:T(2,128)S(1)}, ...), condition=%wide.region_14.14_spmd, body=%wide.region_12.13_spmd.sunk | while | flops 25475176 | bytes 1113291 | solution.py:85
  383.8 2.9 gather_fusion
  388.0 2.9 gather_fusion
  392.1 2.9 gather_fusion
  396.3 2.9 gather_fusion
  405.3 24.9 %while.107 = (s32[]{:T(128)}, f32[48,1,2]{0,2,1:T(2,128)S(1)}, f32[48,1,2,128]{3,0,2,1:T(8,128)S(1)}, s32[]{:T(128)}, s32[]{:T(128)}, /*index=5*/s32[256]{0:T(25...) while((s32[]{:T(128)}, f32[48,1,2]{0,2,1:T(2,128)S(1)}, ...), condition=%wide.region_14.14_spmd, body=%wide.region_12.13_spmd.sunk | while | flops 25475176 | bytes 1113291 | solution.py:85
  406.1 2.9 gather_fusion
  410.2 2.9 gather_fusion
  414.4 2.9 gather_fusion
  418.6 2.9 gather_fusion
  422.7 2.9 gather_fusion
  426.9 2.9 gather_fusion
  435.9 33.2 %while.107 = (s32[]{:T(128)}, f32[48,1,2]{0,2,1:T(2,128)S(1)}, f32[48,1,2,128]{3,0,2,1:T(8,128)S(1)}, s32[]{:T(128)}, s32[]{:T(128)}, /*index=5*/s32[256]{0:T(25...) while((s32[]{:T(128)}, f32[48,1,2]{0,2,1:T(2,128)S(1)}, ...), condition=%wide.region_14.14_spmd, body=%wide.region_12.13_spmd.sunk | while | flops 25475176 | bytes 1113291 | solution.py:85
  436.7 2.9 gather_fusion
  474.8 4.2 while.107
  475.6 2.9 gather_fusion
  484.6 8.3 %while.107 = (s32[]{:T(128)}, f32[48,1,2]{0,2,1:T(2,128)S(1)}, f32[48,1,2,128]{3,0,2,1:T(8,128)S(1)}, s32[]{:T(128)}, s32[]{:T(128)}, /*index=5*/s32[256]{0:T(25...) while((s32[]{:T(128)}, f32[48,1,2]{0,2,1:T(2,128)S(1)}, ...), condition=%wide.region_14.14_spmd, body=%wide.region_12.13_spmd.sunk | while | flops 25475176 | bytes 1113291 | solution.py:85
  498.6 29.1 %while.107 = (s32[]{:T(128)}, f32[48,1,2]{0,2,1:T(2,128)S(1)}, f32[48,1,2,128]{3,0,2,1:T(8,128)S(1)}, s32[]{:T(128)}, s32[]{:T(128)}, /*index=5*/s32[256]{0:T(25...) while((s32[]{:T(128)}, f32[48,1,2]{0,2,1:T(2,128)S(1)}, ...), condition=%wide.region_14.14_spmd, body=%wide.region_12.13_spmd.sunk | while | flops 25475176 | bytes 1113291 | solution.py:85
  515.9 2.9 gather_fusion
  524.3 2.9 gather_fusion
  533.3 20.8 %while.107 = (s32[]{:T(128)}, f32[48,1,2]{0,2,1:T(2,128)S(1)}, f32[48,1,2,128]{3,0,2,1:T(8,128)S(1)}, s32[]{:T(128)}, s32[]{:T(128)}, /*index=5*/s32[256]{0:T(25...) while((s32[]{:T(128)}, f32[48,1,2]{0,2,1:T(2,128)S(1)}, ...), condition=%wide.region_14.14_spmd, body=%wide.region_12.13_spmd.sunk | while | flops 25475176 | bytes 1113291 | solution.py:85
  559.7 33.2 %while.107 = (s32[]{:T(128)}, f32[48,1,2]{0,2,1:T(2,128)S(1)}, f32[48,1,2,128]{3,0,2,1:T(8,128)S(1)}, s32[]{:T(128)}, s32[]{:T(128)}, /*index=5*/s32[256]{0:T(25...) while((s32[]{:T(128)}, f32[48,1,2]{0,2,1:T(2,128)S(1)}, ...), condition=%wide.region_14.14_spmd, body=%wide.region_12.13_spmd.sunk | while | flops 25475176 | bytes 1113291 | solution.py:85
  598.6 8.3 %while.107 = (s32[]{:T(128)}, f32[48,1,2]{0,2,1:T(2,128)S(1)}, f32[48,1,2,128]{3,0,2,1:T(8,128)S(1)}, s32[]{:T(128)}, s32[]{:T(128)}, /*index=5*/s32[256]{0:T(25...) while((s32[]{:T(128)}, f32[48,1,2]{0,2,1:T(2,128)S(1)}, ...), condition=%wide.region_14.14_spmd, body=%wide.region_12.13_spmd.sunk | while | flops 25475176 | bytes 1113291 | solution.py:85
  612.6 20.8 %while.107 = (s32[]{:T(128)}, f32[48,1,2]{0,2,1:T(2,128)S(1)}, f32[48,1,2,128]{3,0,2,1:T(8,128)S(1)}, s32[]{:T(128)}, s32[]{:T(128)}, /*index=5*/s32[256]{0:T(25...) while((s32[]{:T(128)}, f32[48,1,2]{0,2,1:T(2,128)S(1)}, ...), condition=%wide.region_14.14_spmd, body=%wide.region_12.13_spmd.sunk | while | flops 25475176 | bytes 1113291 | solution.py:85
  617.5 2.9 gather_fusion
  639.0 24.9 %while.107 = (s32[]{:T(128)}, f32[48,1,2]{0,2,1:T(2,128)S(1)}, f32[48,1,2,128]{3,0,2,1:T(8,128)S(1)}, s32[]{:T(128)}, s32[]{:T(128)}, /*index=5*/s32[256]{0:T(25...) while((s32[]{:T(128)}, f32[48,1,2]{0,2,1:T(2,128)S(1)}, ...), condition=%wide.region_14.14_spmd, body=%wide.region_12.13_spmd.sunk | while | flops 25475176 | bytes 1113291 | solution.py:85
  648.1 2.9 gather_fusion
  660.5 2.9 gather_fusion
  669.6 33.2 %while.107 = (s32[]{:T(128)}, f32[48,1,2]{0,2,1:T(2,128)S(1)}, f32[48,1,2,128]{3,0,2,1:T(8,128)S(1)}, s32[]{:T(128)}, s32[]{:T(128)}, /*index=5*/s32[256]{0:T(25...) while((s32[]{:T(128)}, f32[48,1,2]{0,2,1:T(2,128)S(1)}, ...), condition=%wide.region_14.14_spmd, body=%wide.region_12.13_spmd.sunk | while | flops 25475176 | bytes 1113291 | solution.py:85
  678.7 2.9 gather_fusion
  691.1 2.9 gather_fusion
  699.4 2.9 gather_fusion
  708.5 29.1 %while.107 = (s32[]{:T(128)}, f32[48,1,2]{0,2,1:T(2,128)S(1)}, f32[48,1,2,128]{3,0,2,1:T(8,128)S(1)}, s32[]{:T(128)}, s32[]{:T(128)}, /*index=5*/s32[256]{0:T(25...) while((s32[]{:T(128)}, f32[48,1,2]{0,2,1:T(2,128)S(1)}, ...), condition=%wide.region_14.14_spmd, body=%wide.region_12.13_spmd.sunk | while | flops 25475176 | bytes 1113291 | solution.py:85
  721.7 2.9 gather_fusion
  730.0 2.9 gather_fusion
  (959 shorter events, 390.7 us)
Async XLA Ops:
  7.2 209.0 %copy-start = (bf16[4608,256]{1,0:T(8,128)(2,1)S(1)}, bf16[4608,256]{1,0:T(8,128)(2,1)}, u32[]{:S(2)}) copy-start(bf16[4608,256]{1,0:T(8,128)(2,1)} %param.25) | copy-start | bytes 7077892
  7.2 163.6 %copy-start.13 = (s32[64]{0:T(128)S(1)}, s32[64]{0:T(128)}, u32[]{:S(2)}) copy-start(s32[64]{0:T(128)} %param.36) | copy-start | bytes 772
  7.2 161.5 %copy-start.7 = (s32[2,256]{1,0:T(2,128)S(1)}, s32[2,256]{1,0:T(2,128)}, u32[]{:S(2)}) copy-start(s32[2,256]{1,0:T(2,128)} %param.35) | copy-start | bytes 6148
  7.2 161.5 %copy-start.8 = (s32[32,2]{0,1:T(2,128)S(1)}, s32[32,2]{0,1:T(2,128)}, u32[]{:S(2)}) copy-start(s32[32,2]{0,1:T(2,128)} %param.34) | copy-start | bytes 772
  7.2 161.7 %copy-start.6 = (s32[16,48]{1,0:T(8,128)S(1)}, s32[16,48]{1,0:T(8,128)}, u32[]{:S(2)}) copy-start(s32[16,48]{1,0:T(8,128)} %param.31) | copy-start | bytes 9220
  7.2 162.4 %copy-start.9 = (s32[1,2]{1,0:T(1,128)S(1)}, s32[1,2]{1,0:T(1,128)}, u32[]{:S(2)}) copy-start(s32[1,2]{1,0:T(1,128)} %param.33) | copy-start | bytes 28
  7.2 162.5 %copy-start.14 = (s32[16]{0:T(128)S(1)}, s32[16]{0:T(128)}, u32[]{:S(2)}) copy-start(s32[16]{0:T(128)} %param.30) | copy-start | bytes 196
  7.2 163.8 %copy-start.10 = (s32[16]{0:T(128)S(1)}, s32[16]{0:T(128)}, u32[]{:S(2)}) copy-start(s32[16]{0:T(128)} %param.32) | copy-start | bytes 196
  7.3 192.7 %all-gather.2.cloned.1.call-start = ((), (), s32[]{:S(2)}) async-start(), calls=%async_computation.1 | async-start | bytes 7962624 | tf_op jit(solution)/shard_map/all_gather | solution.py:125
  158.7 25.4 %all-to-all-start = ((bf16[32,4,16,1,256]{4,2,1,3,0:T(8,128)(2,1)}), bf16[32,4,16,1,256]{4,2,1,3,0:T(8,128)(2,1)}, u32[]{:S(2)}, u32[]{:S(2)}) async-start(bf16[32,4,16,1,256]{4,2,1,3,0:T(8,128)(2,1)} %broadcast_select_fusion), calls=%async_computation | async-start | bytes 2097152 | tf_op jit(solution)/shard_map/all_to_all | solution.py:171
  198.4 6.2 copy-start.12
  198.4 67.0 %collective-permute-start = (bf16[2,4096,1,256]{3,1,2,0:T(8,128)(2,1)}, bf16[2,4096,1,256]{3,1,2,0:T(8,128)(2,1)}, u32[]{:S(2)}, u32[]{:S(2)}) collective-permute-start(bf16[2,4096,1,256]{3,1,2,0:T(8,128)(2,1)} %bitcast.266), channel_id=1, source_target_pairs={{0,8},{8,0},{16,24},{24,16},{32,40},{40,32},{48,56},{56,48},{64,72... | collective-permute-start | bytes 12582920 | tf_op jit(solution)/shard_map/ppermute | solution.py:20
  200.0 5.0 copy-start.1
  205.0 6.4 copy-start.11
  211.4 3.0 copy-start.2
  211.4 3.0 copy-start.4
  214.4 0.7 copy-start.15
  265.4 54.3 %copy-start.3 = (bf16[768,1,64]{2,0,1:T(8,128)(2,1)S(1)}, bf16[768,1,64]{2,0,1:T(8,128)(2,1)}, u32[]{:S(2)}) copy-start(bf16[768,1,64]{2,0,1:T(8,128)(2,1)} %copy-done.2) | copy-start | bytes 294916
  265.4 54.3 %copy-start.5 = (bf16[768,1,64]{2,0,1:T(8,128)(2,1)S(1)}, bf16[768,1,64]{2,0,1:T(8,128)(2,1)}, u32[]{:S(2)}) copy-start(bf16[768,1,64]{2,0,1:T(8,128)(2,1)} %copy-done.4) | copy-start | bytes 294916
Sparse Core Ops, SparseCore 0:
  9.9 47.1 all-gather.1
where the time goes:
time: 759 us; the launch traced here: 746 us
  local copies, waits for them, and re-layouts  310 us (41%)
  blocking collectives  141 us (19%)
  matrix products  117 us (15%)
  other arithmetic  91.6 us (12%)
  waiting for transfers between devices  43.7 us (6%)
  loops' own time  17.7 us (2%)
  between operations  15.1 us (2%)
  starting transfers between devices  10.4 us (1%)
    gather x79, local copies, waits for them, and re-layouts, loader(): gathered = extended[chosen].reshape(block_span, local_heads, 2 * head_size)  230 us
    unnamed x1, blocking collectives  141 us
    lt x94, other arithmetic, advance(): number * block_span + jnp.arange(block_span, dtype=jnp.int32) < length  59.4 us
    dot_general x110, matrix products, absorb(): jnp.einsum('igrd,tgd->igrt', queries, keys_block, preferred_element_type=...  57.1 us
    dot_general x110, matrix products, absorb(): jnp.einsum('igrt,tgd->igrd', weights.astype(jnp.bfloat16), values_block,...  44.9 us
    ppermute x1, waiting for transfers between devices, partner(): return lax.ppermute(value, axis, pairs)  30.2 us
    dynamic_slice x64, local copies, waits for them, and re-layouts, body(): lax.map(request_part, (grouped, keys_grouped, values_grouped, page_table,...  22.7 us
  transfers between devices with their start and end apart: 3, of which 2 were waited for; matrix products, arithmetic and copies ran while one was open for 8% of the time, Pallas kernels for 0%

commit v1 on v0

v1 whole, which is shorter than its diff:
```python
import jax
import jax.numpy as jnp
from jax import lax
from jax.experimental import pallas as pl
from jax.experimental.pallas import tpu as pltpu
from jax.sharding import PartitionSpec as P

CAP = 4
ACCEPT = 5
THETA_LOG = 9.210340371976184
PRE = 144.0 ** (-0.5) / 50.0
LOGIT_CAP = 50.0
POST = 50.0 * 1.4426950408889634
BLOCK_PAGES = 32
F32 = jnp.float32
BF16 = jnp.bfloat16


def nt(a, b):
    return lax.dot_general(a, b, (((1,), (1,)), ((), ())), preferred_element_type=F32)


def nn(a, b):
    return lax.dot_general(a, b, (((1,), (0,)), ((), ())), preferred_element_type=F32)


def weigh(scores):
    return jnp.exp2(jnp.tanh(scores * PRE) * POST)


def fold(weights):
    total = weights[:, 0:128]
    for part in range(1, weights.shape[1] // 128):
        total = total + weights[:, part * 128 : part * 128 + 128]
    return total


def load_pages(pages, table, row, first, count):
    loaded = [pages[table[row, first + number]] for number in range(count)]
    return jnp.concatenate(loaded, 0)


def page_block(query, pages, table, row, first, valid, acc, summed):
    size = pages.shape[1]
    both = load_pages(pages, table, row, first, BLOCK_PAGES)
    weights = weigh(nt(query, both[:, 0:128]))
    if valid is not None:
        where = lax.broadcasted_iota(jnp.int32, (1, BLOCK_PAGES * size), 1)
        weights = jnp.where(where < valid, weights, 0.0)
    summed = summed + fold(weights)
    acc = acc + nn(weights.astype(BF16), both[:, 128:256])
    return acc, summed


def page_loop(query, pages, table, row, length):
    span = BLOCK_PAGES * pages.shape[1]
    zero = jnp.zeros((query.shape[0], 128), F32)

    def step(number, state):
        return page_block(query, pages, table, row, number * BLOCK_PAGES, None, *state)

    full = lax.div(length, span)
    return full, lax.fori_loop(0, full, step, (zero, zero))


def page_rest(query, pages, table, row, full, length, state):
    span = BLOCK_PAGES * pages.shape[1]
    width = table.shape[1]
    first = jnp.minimum(full * BLOCK_PAGES, width - BLOCK_PAGES)
    return page_block(query, pages, table, row, first, length - full * span, *state)


def fill_pages(slots, kv_hbm, moved_hbm, pages, moved, sems):
    pool = kv_hbm.shape[0]
    first = pltpu.make_async_copy(kv_hbm, pages.at[pl.ds(0, pool)], sems.at[0])
    second = pltpu.make_async_copy(moved_hbm, moved, sems.at[1])
    first.start()
    second.start()
    first.wait()
    second.wait()
    for number in range(slots.shape[0]):
        pages[pool + number] = moved[slots[number]]


def far_kernel(slots, table, lens, kv_hbm, moved_hbm, q_ref, acc_ref, sum_ref, pages, moved, sems):
    fill_pages(slots, kv_hbm, moved_hbm, pages, moved, sems)
    for j in range(q_ref.shape[0]):
        query = q_ref[j]
        full, state = page_loop(query, pages, table, j, lens[j])
        acc, summed = page_rest(query, pages, table, j, full, lens[j], state)
        acc_ref[j] = acc
        sum_ref[j] = summed


def own_kernel(
    slots, table, lens, pair, leaf, kv_hbm, moved_hbm, q_ref, new_ref, mask_ref, facc_ref, fsum_ref,
    out_ref, path_ref, pages, moved, sems,
):
    fill_pages(slots, kv_hbm, moved_hbm, pages, moved, sems)
    tree = mask_ref.shape[1]

    def request(r, carry):
        rows = pl.ds(pl.multiple_of(r * tree, tree), tree)
        query = jnp.concatenate([q_ref[rows, 0:128], q_ref[rows, 128:256]], 0)
        length = lens[r]
        full, state = page_loop(query, pages, table, r, length)
        acc, summed = page_rest(query, pages, table, r, full, length, state)
        new = new_ref[rows, :]
        mask = mask_ref[r]
        weights = weigh(nt(query, new[:, 0:128])) * jnp.concatenate([mask, mask], 0)
        acc = acc + nn(weights.astype(BF16), new[:, 128:256])
        for j in range(2):
            mine = jnp.where(pair[0, j] == r, 1.0, 0.0)
            acc = acc + mine * facc_ref[j]
            summed = summed + mine * fsum_ref[j]
        total = jnp.sum(summed, -1, keepdims=True) + jnp.sum(weights, -1, keepdims=True)
        mixed = (acc / total).astype(BF16)
        out_ref[rows, 0:128] = mixed[0:tree]
        out_ref[rows, 128:256] = mixed[tree:]
        ones = jnp.ones((8, tree), F32)
        depth = nt(ones.astype(BF16), mask.astype(BF16)) - 1.0
        levels = lax.broadcasted_iota(jnp.int32, (8, tree), 0).astype(F32)
        lineage = mask_ref[r, pl.ds(leaf[r], 1), :]
        picker = jnp.where(depth == levels, 1.0, 0.0) * lineage
        path_ref[r] = nn(picker.astype(BF16), new).astype(BF16)
        return carry

    lax.fori_loop(0, lens.shape[0], request, 0)


def smem():
    return pl.BlockSpec(memory_space=pltpu.SMEM)


def anyspace():
    return pl.BlockSpec(memory_space=pl.ANY)


def vmem():
    return pl.BlockSpec(memory_space=pltpu.VMEM)


def page_scratch(kv, moved, slots):
    return [
        pltpu.VMEM((kv.shape[0] + slots.shape[0],) + kv.shape[1:], BF16),
        pltpu.VMEM(moved.shape, BF16),
        pltpu.SemaphoreType.DMA((2,)),
    ]


def attend_far(slots, table, lens, kv, moved, queries):
    shape = jax.ShapeDtypeStruct(queries.shape, F32)
    return pl.pallas_call(
        far_kernel,
        out_shape=(shape, shape),
        in_specs=[smem(), smem(), smem(), anyspace(), anyspace(), vmem()],
        out_specs=(vmem(), vmem()),
        scratch_shapes=page_scratch(kv, moved, slots),
        compiler_params=pltpu.CompilerParams(vmem_limit_bytes=40 << 20),
        name="attend_far",
    )(slots, table, lens, kv, moved, queries)


def attend_own(slots, table, lens, pair, leaf, kv, moved, queries, fresh, mask, facc, fsum):
    requests = lens.shape[0]
    return pl.pallas_call(
        own_kernel,
        out_shape=(
            jax.ShapeDtypeStruct(queries.shape, BF16),
            jax.ShapeDtypeStruct((requests, 8, 256), BF16),
        ),
        in_specs=[smem()] * 5 + [anyspace(), anyspace()] + [vmem()] * 5,
        out_specs=(vmem(), vmem()),
        scratch_shapes=page_scratch(kv, moved, slots),
        compiler_params=pltpu.CompilerParams(vmem_limit_bytes=40 << 20),
        name="attend_own",
    )(slots, table, lens, pair, leaf, kv, moved, queries, fresh, mask, facc, fsum)


def partner(value, axis):
    pairs = [(source, source ^ 1) for source in range(lax.axis_size(axis))]
    return lax.ppermute(value, axis, pairs)


def rotate(values, position):
    halfway = values.shape[-1] // 2
    angles = jnp.exp(-THETA_LOG * 2.0 * jnp.arange(halfway, dtype=F32) / values.shape[-1])
    phases = position.astype(F32)[:, None] * angles[None, :]
    cosine = jnp.cos(phases)[:, None, :]
    sine = jnp.sin(phases)[:, None, :]
    former = values[..., :halfway]
    latter = values[..., halfway:]
    return jnp.concatenate([former * cosine - latter * sine, latter * cosine + former * sine], -1)


def ancestry(parents):
    length = parents.shape[-1]
    labels = jnp.arange(length, dtype=jnp.int32)
    reached = (parents[..., :, None] == labels).astype(BF16) + jnp.eye(length, dtype=BF16)
    for _ in range(2):
        reached = jnp.minimum(
            jnp.einsum("nij,njk->nik", reached, reached, preferred_element_type=F32), 1.0
        ).astype(BF16)
    reached = reached.astype(F32)
    depths = jnp.sum(reached, -1).astype(jnp.int32) - 1
    return reached, depths


def body(
    hidden, norm_gain, q_weight, k_weight, v_weight, kv_pages, page_table, cache_len, tree_parent,
    accept_node, pair_slot, far_len, far_table, mig_src, mig_page,
):
    token_rows = hidden.shape[0]
    requests, tree = tree_parent.shape
    pool, page_size, _, entry = kv_pages.shape
    migrations = mig_src.shape[0]
    groups = lax.axis_size("grp")
    myself = lax.axis_index("grp")
    kv = kv_pages.reshape(pool, page_size, entry)
    order = jnp.arange(migrations, dtype=jnp.int32)
    rank = jnp.sum(
        ((mig_src[:, None] == mig_src[None, :]) & (order[:, None] > order[None, :])).astype(jnp.int32), -1
    )
    slots = mig_src * CAP + rank
    wanted = jnp.max(
        jnp.where(
            slots[None, :] == jnp.arange(groups * CAP, dtype=jnp.int32)[:, None], mig_page[None, :], 0
        ),
        -1,
    ).reshape(groups, CAP)
    asked = lax.all_to_all(wanted, "grp", split_axis=0, concat_axis=0, tiled=True)
    outgoing = kv[asked.reshape(-1)].reshape(groups, CAP, page_size, entry)
    moved = lax.all_to_all(outgoing, "grp", split_axis=0, concat_axis=0, tiled=True)
    moved = moved.reshape(groups * CAP, page_size, entry)
    widened = lax.all_gather(hidden, "tp", axis=1, tiled=True).astype(F32)
    scaled = (widened * norm_gain[None, :]).astype(BF16)
    row_scale = lax.rsqrt(jnp.mean(widened * widened, 1) + 1e-06)[:, None]
    reached, depths = ancestry(tree_parent)
    far_mine = lax.dynamic_index_in_dim(far_len, myself, 0, keepdims=False)
    far_theirs = lax.dynamic_index_in_dim(far_len, myself ^ 1, 0, keepdims=False)
    matched = jnp.arange(requests, dtype=jnp.int32)[:, None] == pair_slot
    far_own = jnp.sum(jnp.where(matched, far_mine[None, :], 0), 1)
    position = ((cache_len + far_own)[:, None] + depths).reshape(-1)
    dot = lambda weight: jnp.dot(scaled, weight, preferred_element_type=F32) * row_scale
    queries = rotate(dot(q_weight).reshape(token_rows, 2, 128), position)
    queries = queries.astype(BF16).reshape(token_rows, 256)
    keys_new = rotate(dot(k_weight).reshape(token_rows, 1, 128), position)
    keys_new = keys_new.astype(BF16).reshape(token_rows, 128)
    fresh = jnp.concatenate([keys_new, dot(v_weight).astype(BF16)], 1)
    long_queries = queries.reshape(requests, tree, 2, 128).transpose(0, 2, 1, 3)
    long_queries = long_queries.reshape(requests, 2 * tree, 128)[pair_slot[0]]
    visitors = partner(long_queries, "grp")
    facc, fsum = attend_far(slots, far_table, far_theirs, kv, moved, visitors)
    facc = partner(facc, "grp")
    fsum = partner(fsum, "grp")
    out, path = attend_own(
        slots, page_table, cache_len, pair_slot, accept_node, kv, moved, queries, fresh, reached, facc, fsum
    )
    return out, path[:, :ACCEPT].reshape(requests * ACCEPT, 1, entry)


def solution(mesh):
    in_specs = (
        P("grp", "tp"),
        P(),
        P(None, "tp"),
        P(None, "tp"),
        P(None, "tp"),
        P("grp", None, "tp", None),
        P("grp", None),
        P("grp"),
        P("grp", None),
        P("grp"),
        P("grp", None),
        P(),
        P("grp", None),
        P("grp"),
        P("grp"),
    )
    out_specs = (P("grp", "tp"), P("grp", "tp", None))
    return jax.shard_map(body, mesh=mesh, in_specs=in_specs, out_specs=out_specs, check_vma=False)
```

time: 759 us -> 162 us (0.21)
  the two profiles are of different devices: /device:TPU:132 before, /device:TPU:120 now
where the time goes in v1:
time: 162 us; the launch traced here: 161 us
  Pallas kernels  43.7 us (27%)
  local copies, waits for them, and re-layouts  24.2 us (15%)
  starting transfers between devices  23.1 us (14%)
  waiting for transfers between devices  19.2 us (12%)
  other arithmetic  18.9 us (12%)
  matrix products  17.4 us (11%)
  between operations  14.3 us (9%)
    pallas_call x1, Pallas kernels, attend_own(): pl.pallas_call(own_kernel, out_shape=(jax.ShapeDtypeStruct(queries.shape,...  36.9 us
    all_gather x1, waiting for transfers between devices, body(): widened = lax.all_gather(hidden, 'tp', axis=1, tiled=True).astype(F32)  15 us
    dot_general x3, matrix products, body(): jnp.dot(scaled, weight, preferred_element_type=F32) * row_scale  15 us
    all_to_all x1, starting transfers between devices, body(): lax.all_to_all(wanted, 'grp', split_axis=0, concat_axis=0, tiled=True)  10.1 us
    all_to_all x1, starting transfers between devices, body(): lax.all_to_all(outgoing, 'grp', split_axis=0, concat_axis=0, tiled=True)  9.77 us
    concatenate x4, local copies, waits for them, and re-layouts, rotate(): jnp.concatenate([former * cosine - latter * sine, latter * cosine + forme...  9.29 us
    pallas_call x1, Pallas kernels, attend_far(): pl.pallas_call(far_kernel, out_shape=(shape, shape), in_specs=[smem(), sm...  6.77 us
    concatenate x3, other arithmetic, rotate(): jnp.concatenate([former * cosine - latter * sine, latter * cosine + forme...  5.41 us
  transfers between devices with their start and end apart: 6, of which 3 were waited for; matrix products, arithmetic and copies ran while one was open for 34% of the time, Pallas kernels for 0%

profile of v1, /device:TPU:120, one launch (start us, length us, event | category | flops | bytes accessed | tf_op | source)
XLA Modules:
  0.0 160.8 jit_solution(5475236868024092880)
XLA Ops:
  7.2 0.0 copy-start
  7.2 0.0 copy-start.15
  7.2 0.0 all-gather.2.cloned.1.call-start
  7.2 0.7 all-gather.2.cloned.1.call-update
  7.9 0.9 convert_reduce_fusion
  8.8 0.7 multiply_add_fusion.slots
  9.5 0.7 select_reduce_fusion
  10.3 0.7 all_to_all.9
  11.0 10.1 %all-to-all-start = ((s32[32,1,4]{2,1,0:T(1,128)}), s32[32,1,4]{2,1,0:T(1,128)S(1)}, u32[]{:S(2)}, u32[]{:S(2)}) async-start(s32[32,1,4]{2,1,0:T(1,128)} %bitcast.1), calls=%async_computation | async-start | bytes 32768 | tf_op jit(solution)/shard_map/all_to_all | solution.py:231
  21.1 1.0 dynamic-slice_reduce_fusion
  22.1 0.8 fusion.28
  22.8 0.7 add.87
  23.5 2.4 %fusion.35 = (f32[16,48]{1,0:T(8,128)S(1)}, f32[16,48,48]{2,1,0:T(8,128)}) fusion(s32[16,48]{1,0:T(8,128)} %param.23, bf16[48,48]{1,0:T(8,128)(2,1)S(1)} %fusion.27), kind=kOutput, calls=%fused_computation.63 | convolution fusion | flops 7519488 | bytes 158208 | tf_op jit(solution)/shard_map/nij,njk->nik/dot_general | solution.py:202
  25.9 0.1 add_convert_fusion.1
  25.9 0.1 convert_element_type.71
  26.0 0.7 fusion.30
  26.7 1.6 multiply_cosine_fusion.1
  28.3 0.0 all-to-all-done
  28.3 0.5 broadcast.163
  28.8 0.7 reduce.7
  29.5 0.1 reshape.249
  29.6 3.8 %gather_fusion = bf16[128,16,256]{2,1,0:T(8,128)(2,1)} fusion(bf16[512,16,256]{2,1,0:T(8,128)(2,1)} %bitcast.30, s32[1024]{0:T(1024)S(1)} %pad_clamp_fusion.1), kind=kCustom, calls=%fused_computation | custom fusion | bytes 2097664 | tf_op jit(solution)/shard_map/gather | solution.py:232
  33.4 9.8 %all-to-all-start.1 = ((bf16[32,4,16,256]{3,2,1,0:T(8,128)(2,1)}), bf16[32,4,16,256]{3,2,1,0:T(8,128)(2,1)S(1)}, u32[]{:S(2)}, u32[]{:S(2)}) async-start(bf16[32,4,16,256]{3,2,1,0:T(8,128)(2,1)} %bitcast.37), calls=%async_computation.1 | async-start | bytes 2097152 | tf_op jit(solution)/shard_map/all_to_all | solution.py:233
  43.2 15.0 %all-gather.2.cloned.1.call-done = bf16[768,4608]{0,1:T(8,128)(2,1)} async-done(((bf16[768,576]{0,1:T(8,128)(2,1)}), bf16[768,4608]{0,1:T(8,128)(2,1)}) %all-gather.2.cloned.1.call-update) | async-done | bytes 7077904 | tf_op jit(solution)/shard_map/all_gather | solution.py:235
  58.2 4.6 %fusion.1 = f32[768]{0:T(1024)S(1)} fusion(bf16[768,4608]{0,1:T(8,128)(2,1)} %all-gather.2.cloned.1.call-done), kind=kLoop, calls=%fused_computation.5 | loop fusion | flops 10616064 | bytes 7080960 | tf_op jit(solution)/shard_map/reduce_sum | solution.py:237
  62.9 0.0 copy-done
  62.9 0.0 copy-done.15
  62.9 0.4 copy-done.9
  63.3 2.6 %convolution_multiply_fusion = f32[768,256]{0,1:T(8,128)S(1)} fusion(bf16[4608,256]{1,0:T(8,128)(2,1)S(1)} %copy-done, f32[768]{0:T(1024)S(1)} %add_rsqrt_fusion, bf16[768,4608]{0,1:T(8,128)(2,1)S(1)} %copy-done.9, f32[4608]{0:T(1024)S(1)} %copy-done.15), kind=kOutput, calls=%fused_computation.6 | convolution fusion | flops 1822752768 | bytes 10245120 | tf_op jit(solution)/shard_map/dot_general | solution.py:244
  65.8 0.0 copy-done.12
  65.9 0.8 subtract_convert_fusion
  66.7 2.4 %concatenate.29 = bf16[16,48,2,64]{1,0,3,2:T(8,128)(2,1)} reshape(bf16[768,2,64]{0,2,1:T(8,128)(2,1)} %get-tuple-element.12) | data formatting | bytes 393216 | tf_op jit(solution)/shard_map/concatenate | solution.py:193
  69.1 2.2 %copy.49 = bf16[16,48,2,64]{3,1,2,0:T(8,128)(2,1)} copy(bf16[16,48,2,64]{1,0,3,2:T(8,128)(2,1)} %concatenate.29) | data formatting | bytes 393216 | tf_op jit(solution)/shard_map/concatenate | solution.py:193
  71.4 2.4 %concatenate.30 = bf16[16,48,2,64]{1,0,3,2:T(8,128)(2,1)} reshape(bf16[768,2,64]{0,2,1:T(8,128)(2,1)} %get-tuple-element.13) | data formatting | bytes 393216 | tf_op jit(solution)/shard_map/concatenate | solution.py:193
  73.8 2.2 %copy.50 = bf16[16,48,2,64]{3,1,2,0:T(8,128)(2,1)} copy(bf16[16,48,2,64]{1,0,3,2:T(8,128)(2,1)} %concatenate.30) | data formatting | bytes 393216 | tf_op jit(solution)/shard_map/concatenate | solution.py:193
  76.0 2.1 %pad_maximum_fusion.2 = bf16[16,48,2,128]{3,1,2,0:T(8,128)(2,1)} fusion(bf16[16,48,2,64]{3,1,2,0:T(8,128)(2,1)} %copy.50, bf16[16,48,2,64]{3,1,2,0:T(8,128)(2,1)} %copy.49), kind=kLoop, calls=%fused_computation.28 | loop fusion | flops 786432 | bytes 786432 | tf_op jit(solution)/shard_map/concatenate | solution.py:193
  78.1 1.6 gather_fusion.1
  79.7 0.0 copy-start.14
  79.7 1.1 collective-permute-start
  80.8 6.0 %fusion.2 = f32[768,1,128]{2,0,1:T(8,128)S(1)} fusion(bf16[4608,128]{1,0:T(8,128)(2,1)} %param.18, f32[768]{0:T(1024)S(1)} %add_rsqrt_fusion, bf16[768,4608]{0,1:T(8,128)(2,1)} %all-gather.2.cloned.1.call-done, f32[4608]{0:T(1024)} %param.16), kind=kOutput, calls=%fused_computation.11 | convolution fusion | flops 916684800 | bytes 8672256 | tf_op jit(solution)/shard_map/dot_general | solution.py:244
  86.8 2.5 %fusion.23 = (bf16[768,64]{1,0:T(8,128)(2,1)}, bf16[768,64]{1,0:T(8,128)(2,1)}) fusion(f32[768,1,128]{2,0,1:T(8,128)S(1)} %fusion.2, f32[64]{0:T(128)S(1)} %multiply_exponential_fusion, f32[768]{0:T(1024)S(1)} %convert_element_type.71), kind=kLoop, calls=%fused_computation.39 | loop fusion | flops 442368 | bytes 593152 | tf_op jit(solution)/shard_map/concatenate | solution.py:193
  89.3 0.0 copy-done.14
  89.3 6.5 %fusion.3 = bf16[768,128]{1,0:T(8,128)(2,1)} fusion(bf16[4608,128]{1,0:T(8,128)(2,1)S(1)} %copy-done.14, f32[768]{0:T(1024)S(1)} %add_rsqrt_fusion, bf16[768,4608]{0,1:T(8,128)(2,1)} %all-gather.2.cloned.1.call-done, f32[4608]{0:T(1024)} %param.16), kind=kOutput, calls=%fused_computation.12 | convolution fusion | flops 916783104 | bytes 8475648 | tf_op jit(solution)/shard_map/dot_general | solution.py:244
  95.8 0.0 copy-done.11
  95.8 0.0 copy-start.6
  95.8 0.0 copy-start.7
  95.8 0.0 copy-start.8
  95.9 0.8 pad_maximum_fusion
  96.6 1.9 %copy.55.q_ref = bf16[768,256]{1,0:T(8,128)(2,1)} copy(bf16[768,256]{0,1:T(8,128)(2,1)} %bitcast.38) | data formatting | bytes 786432 | tf_op jit(solution)/shard_map/convert_element_type | solution.py:246
  98.5 0.0 all-to-all-done.1
  98.5 0.0 collective-permute-done.q_ref
  98.5 0.0 copy-start.1
  98.5 2.2 %copy-done.1 = bf16[512,16,1,256]{3,1,2,0:T(8,128)(2,1)S(1)} copy-done((bf16[512,16,1,256]{3,1,2,0:T(8,128)(2,1)S(1)}, bf16[512,16,1,256]{3,1,2,0:T(8,128)(2,1)}, u32[]{:S(2)}) %copy-start.1) | copy-done | bytes 4194328
  100.7 6.8 %attend_far.1 = (f32[2,96,128]{2,1,0:T(8,128)S(1)}, f32[2,96,128]{2,1,0:T(8,128)S(1)}) custom-call(s32[64]{0:T(128)S(1)} %multiply_add_fusion.slots, s32[2,256]{1,0:T(2,128)S(1)} %copy-done.5, s32[2]{0:T(128)S(1)} %get-tuple-element.10.lens, bf16[512,16,256]{2,1,0:T(8,128)(2,1)S(1)} %bitcast.31, bf16[128,16,256]{2,1,0:T(8,128)(2,1)S(1)} %bitcast.33, ...), custom_call_target="tpu_custom_call" | custom-call | tf_op jit(solution)/shard_map/attend_far/pallas_call | solution.py:153
  107.5 0.9 collective-permute-start.1
  108.4 1.2 collective-permute-start.2
  109.6 1.3 pad_maximum_fusion.1.new_ref
  110.9 2.3 %collective-permute-done.1.facc_ref = f32[2,96,128]{2,1,0:T(8,128)S(1)} collective-permute-done((f32[2,96,128]{2,1,0:T(8,128)S(1)}, f32[2,96,128]{2,1,0:T(8,128)S(1)}, u32[]{:S(2)}, u32[]{:S(2)}) %collective-permute-start.1) | collective-permute-done | bytes 98336 | tf_op jit(solution)/shard_map/ppermute | solution.py:182
  113.3 1.1 collective-permute-done.2.fsum_ref
  114.4 0.0 copy-done.4
  114.4 1.0 copy-done.2
  115.4 1.0 copy-done.3
  116.4 36.9 %attend_own.1 = (bf16[768,256]{1,0:T(8,128)(2,1)}, bf16[16,8,256]{2,1,0:T(8,128)(2,1)S(1)}) custom-call(s32[64]{0:T(128)S(1)} %multiply_add_fusion.slots, s32[16,256]{1,0:T(8,128)S(1)} %copy-done.4, s32[16]{0:T(128)S(1)} %copy-done.6, s32[1,2]{1,0:T(1,128)S(1)} %copy-done.7, s32[16]{0:T(128)S(1)} %copy-done.8, bf16[512,16,256]{2,1,0:T(8,128)(2,1)S(1)} %bitcast.32, ...), custom_call_target="tpu_custom_call" | custom-call | tf_op jit(solution)/shard_map/attend_own/pallas_call | solution.py:166
  153.3 0.6 reshape.255
  (21 shorter events, 0.1 us)
Async XLA Ops:
  7.2 55.7 %copy-start = (bf16[4608,256]{1,0:T(8,128)(2,1)S(1)}, bf16[4608,256]{1,0:T(8,128)(2,1)}, u32[]{:S(2)}) copy-start(bf16[4608,256]{1,0:T(8,128)(2,1)} %param.17) | copy-start | bytes 7077892
  7.2 55.7 %copy-start.15 = (f32[4608]{0:T(1024)S(1)}, f32[4608]{0:T(1024)}, u32[]{:S(2)}) copy-start(f32[4608]{0:T(1024)} %param.16) | copy-start | bytes 55300
  7.2 51.0 %all-gather.2.cloned.1.call-start = ((), (), s32[]{:S(2)}) async-start(), calls=%async_computation.2 | async-start | bytes 7962624 | tf_op jit(solution)/shard_map/all_gather | solution.py:235
  11.0 17.3 %all-to-all-start = ((s32[32,1,4]{2,1,0:T(1,128)}), s32[32,1,4]{2,1,0:T(1,128)S(1)}, u32[]{:S(2)}, u32[]{:S(2)}) async-start(s32[32,1,4]{2,1,0:T(1,128)} %bitcast.1), calls=%async_computation | async-start | bytes 32768 | tf_op jit(solution)/shard_map/all_to_all | solution.py:231
  33.4 65.1 %all-to-all-start.1 = ((bf16[32,4,16,256]{3,2,1,0:T(8,128)(2,1)}), bf16[32,4,16,256]{3,2,1,0:T(8,128)(2,1)S(1)}, u32[]{:S(2)}, u32[]{:S(2)}) async-start(bf16[32,4,16,256]{3,2,1,0:T(8,128)(2,1)} %bitcast.37), calls=%async_computation.1 | async-start | bytes 2097152 | tf_op jit(solution)/shard_map/all_to_all | solution.py:233
  58.2 5.0 %copy-start.9 = (bf16[768,4608]{0,1:T(8,128)(2,1)S(1)}, bf16[768,4608]{0,1:T(8,128)(2,1)}, u32[]{:S(2)}) copy-start(bf16[768,4608]{0,1:T(8,128)(2,1)} %all-gather.2.cloned.1.call-done) | copy-start | bytes 21233668
  63.3 2.6 %copy-start.12 = (f32[768,64]{0,1:T(8,128)S(1)}, f32[768,64]{0,1:T(8,128)}, u32[]{:S(2)}) copy-start(f32[768,64]{0,1:T(8,128)} %get-tuple-element.16) | copy-start | bytes 589828
  63.3 2.6 %copy-start.13 = (f32[768,64]{0,1:T(8,128)S(1)}, f32[768,64]{0,1:T(8,128)}, u32[]{:S(2)}) copy-start(f32[768,64]{0,1:T(8,128)} %get-tuple-element.17) | copy-start | bytes 589828
  79.7 9.6 %copy-start.14 = (bf16[4608,128]{1,0:T(8,128)(2,1)S(1)}, bf16[4608,128]{1,0:T(8,128)(2,1)}, u32[]{:S(2)}) copy-start(bf16[4608,128]{1,0:T(8,128)(2,1)} %param.19) | copy-start | bytes 3538948
  79.7 18.8 %collective-permute-start = (bf16[2,96,128]{2,1,0:T(8,128)(2,1)S(1)}, bf16[2,96,128]{2,1,0:T(8,128)(2,1)S(1)}, u32[]{:S(2)}, u32[]{:S(2)}) collective-permute-start(bf16[2,96,128]{2,1,0:T(8,128)(2,1)S(1)} %gather_fusion.1), channel_id=1, source_target_pairs={{0,8},{8,0},{16,24},{24,16},{32,40},{40,32},{48,56},{56,48},{64,72... | collective-permute-start | bytes 147464 | tf_op jit(solution)/shard_map/ppermute | solution.py:182
  86.8 9.0 %copy-start.10 = (bf16[768,2,64]{0,2,1:T(8,128)(2,1)S(1)}, bf16[768,2,64]{0,2,1:T(8,128)(2,1)}, u32[]{:S(2)}) copy-start(bf16[768,2,64]{0,2,1:T(8,128)(2,1)} %get-tuple-element.12) | copy-start | bytes 589828
  86.8 9.0 %copy-start.11 = (bf16[768,2,64]{0,2,1:T(8,128)(2,1)S(1)}, bf16[768,2,64]{0,2,1:T(8,128)(2,1)}, u32[]{:S(2)}) copy-start(bf16[768,2,64]{0,2,1:T(8,128)(2,1)} %get-tuple-element.13) | copy-start | bytes 589828
  89.3 9.2 %copy-start.5 = (s32[2,256]{1,0:T(2,128)S(1)}, s32[2,256]{1,0:T(2,128)}, u32[]{:S(2)}) copy-start(s32[2,256]{1,0:T(2,128)} %table.2) | copy-start | bytes 6148
  95.8 18.6 %copy-start.4 = (s32[16,256]{1,0:T(8,128)S(1)}, s32[16,256]{1,0:T(8,128)}, u32[]{:S(2)}) copy-start(s32[16,256]{1,0:T(8,128)} %table.3) | copy-start | bytes 49156
  95.8 18.6 %copy-start.6 = (s32[16]{0:T(128)S(1)}, s32[16]{0:T(128)}, u32[]{:S(2)}) copy-start(s32[16]{0:T(128)} %lens.1) | copy-start | bytes 196
  95.8 18.6 %copy-start.7 = (s32[1,2]{1,0:T(1,128)S(1)}, s32[1,2]{1,0:T(1,128)}, u32[]{:S(2)}) copy-start(s32[1,2]{1,0:T(1,128)} %pair.1) | copy-start | bytes 28
  95.8 18.5 %copy-start.8 = (s32[16]{0:T(128)S(1)}, s32[16]{0:T(128)}, u32[]{:S(2)}) copy-start(s32[16]{0:T(128)} %leaf.1) | copy-start | bytes 196
  98.5 2.2 %copy-start.1 = (bf16[512,16,1,256]{3,1,2,0:T(8,128)(2,1)S(1)}, bf16[512,16,1,256]{3,1,2,0:T(8,128)(2,1)}, u32[]{:S(2)}) copy-start(bf16[512,16,1,256]{3,1,2,0:T(8,128)(2,1)} %param.20) | copy-start | bytes 12582916
  107.5 5.7 %collective-permute-start.1 = (f32[2,96,128]{2,1,0:T(8,128)S(1)}, f32[2,96,128]{2,1,0:T(8,128)S(1)}, u32[]{:S(2)}, u32[]{:S(2)}) collective-permute-start(f32[2,96,128]{2,1,0:T(8,128)S(1)} %get-tuple-element.6), channel_id=1, source_target_pairs={{0,8},{8,0},{16,24},{24,16},{32,40},{40,32},{48,56},{56,48},{64,72... | collective-permute-start | bytes 294920 | tf_op jit(solution)/shard_map/ppermute | solution.py:182
  108.4 6.0 %collective-permute-start.2 = (f32[2,96,128]{2,1,0:T(8,128)S(1)}, f32[2,96,128]{2,1,0:T(8,128)S(1)}, u32[]{:S(2)}, u32[]{:S(2)}) collective-permute-start(f32[2,96,128]{2,1,0:T(8,128)S(1)} %get-tuple-element.7), channel_id=1, source_target_pairs={{0,8},{8,0},{16,24},{24,16},{32,40},{40,32},{48,56},{56,48},{64,72... | collective-permute-start | bytes 294920 | tf_op jit(solution)/shard_map/ppermute | solution.py:182
  114.4 1.0 copy-start.2
  115.4 1.0 copy-start.3
Sparse Core Ops, SparseCore 0:
  9.9 48.3 all-gather.1

commit v2 on v1

v2 whole, which is shorter than its diff:
```python
import functools

import jax
import jax.numpy as jnp
from jax import lax
from jax.experimental import pallas as pl
from jax.experimental.pallas import tpu as pltpu
from jax.sharding import PartitionSpec as P

CAP = 4
ACCEPT = 5
THETA_LOG = 9.210340371976184
PRE = 144.0 ** (-0.5) / 50.0
POST = 50.0 * 1.4426950408889634
PARTS = 4
ITEM_PAGES = 64
EARLY = 4
F32 = jnp.float32
BF16 = jnp.bfloat16
I32 = jnp.int32
MESH = pl.DeviceIdType.MESH


def nt(a, b):
    return lax.dot_general(a, b, (((1,), (1,)), ((), ())), preferred_element_type=F32)


def nn(a, b):
    return lax.dot_general(a, b, (((1,), (0,)), ((), ())), preferred_element_type=F32)


def tn(a, b):
    return lax.dot_general(a, b, (((0,), (0,)), ((), ())), preferred_element_type=F32)


def weigh(scores):
    return jnp.exp2(jnp.tanh(scores * PRE) * POST)


def kernel(
    groups, share,
    table_hbm, lens_hbm, pair_hbm, leaf_hbm, far_len_hbm, far_table_hbm, src_hbm, page_hbm, gain_hbm, parents_hbm,
    hidden, kv_hbm, q_hbm, k_hbm, v_hbm,
    out, path,
    table, lens, pair, leaf, far_len, far_table, own_src, own_page, gain_rows, parents,
    tables, landed, wish, wish_smem, gain, xbuf, weights, acc, squares, xs, cosine, sine, pages, packed, arrived,
    masks, pickers, queries, fresh, scores, values, mixed, sums, far_query, far_ask, far_reply, far_back, row_reply,
    row_back,
    small_sem, local_sem, send_sem, recv_sem, table_send, table_recv, page_send, page_recv, far_send, far_recv,
):
    group = lax.axis_index("grp")
    me = lax.axis_index("tp")
    chips = share // 2
    chip, core = me // 2, me % 2
    right = ((chip + 1) % chips) * 2 + core
    left = ((chip + chips - 1) % chips) * 2 + core
    across = ((chip + 2) % chips) * 2 + core
    sibling = chip * 2 + 1 - core
    others = groups - 1
    mate = group + 1 - 2 * (group % 2)
    width, tokens = hidden.shape
    piece = width // PARTS
    pool, size = kv_hbm.shape[0:2]
    requests, tree = parents.shape
    migrations = own_src.shape[1]

    small = [
        pltpu.make_async_copy(source, target, small_sem.at[number])
        for number, (source, target) in enumerate(
            (
                (src_hbm, own_src),
                (page_hbm, own_page),
                (gain_hbm, gain_rows),
                (parents_hbm, parents),
                (table_hbm, table),
                (lens_hbm, lens),
                (pair_hbm, pair),
                (leaf_hbm, leaf),
                (far_len_hbm, far_len),
                (far_table_hbm, far_table),
            )
        )
    ]
    loads = [
        pltpu.make_async_copy(hidden, xbuf.at[me], local_sem.at[0]),
        pltpu.make_async_copy(kv_hbm, pages.at[pl.ds(0, pool)], local_sem.at[1]),
        pltpu.make_async_copy(q_hbm, weights.at[:, pl.ds(0, 256)], local_sem.at[2]),
        pltpu.make_async_copy(k_hbm, weights.at[:, pl.ds(256, 128)], local_sem.at[3]),
        pltpu.make_async_copy(v_hbm, weights.at[:, pl.ds(384, 128)], local_sem.at[4]),
    ]
    small[0].start()
    small[1].start()

    barrier = pltpu.get_barrier_semaphore()
    for peer in (left, right, sibling):
        pl.semaphore_signal(barrier, inc=1, device_id=(group, peer), device_id_type=MESH)

    def greet(number, carry):
        peer = (group + 1 + number) % groups
        pl.semaphore_signal(barrier, inc=1, device_id=(peer, me), device_id_type=MESH)
        return carry

    lax.fori_loop(0, others, greet, 0)
    small[0].wait()
    small[1].wait()
    tables[:, 0:migrations] = own_src[...]
    tables[:, migrations : 2 * migrations] = own_page[...]
    pl.semaphore_wait(barrier, 3 + others)

    sent = []

    def send(source, owner, part, peer):
        copy = pltpu.make_async_remote_copy(
            src_ref=source,
            dst_ref=xbuf.at[owner, pl.ds(part * piece, piece)],
            send_sem=send_sem.at[len(sent)],
            recv_sem=recv_sem.at[owner, part],
            device_id=(group, peer),
            device_id_type=MESH,
        )
        copy.start()
        sent.append(copy)

    def own_part(part):
        return hidden.at[pl.ds(part * piece, piece)]

    def held(owner, part):
        return xbuf.at[owner, pl.ds(part * piece, piece)]

    def arrive(owner, part):
        pltpu.make_async_remote_copy(
            src_ref=held(owner, part),
            dst_ref=held(owner, part),
            send_sem=send_sem.at[0],
            recv_sem=recv_sem.at[owner, part],
            device_id=(group, sibling),
            device_id_type=MESH,
        ).wait_recv()

    def table_copy(number):
        return pltpu.make_async_remote_copy(
            src_ref=tables,
            dst_ref=landed.at[number],
            send_sem=table_send,
            recv_sem=table_recv,
            device_id=((group + 1 + number) % groups, me),
            device_id_type=MESH,
        )

    def tell(number, carry):
        table_copy(number).start()
        return carry

    for part in range(PARTS):
        send(own_part(part), me, part, right)
        send(own_part(PARTS - 1 - part), me, PARTS - 1 - part, left)
        if part == 0:
            lax.fori_loop(0, others, tell, 0)
    for part in range(PARTS):
        send(own_part(part), me, part, sibling)
    for copy in loads + small[2:]:
        copy.start()

    def blank():
        pages[pl.ds(pool, migrations)] = jnp.zeros((migrations,) + pages.shape[1:], BF16)
        acc[...] = jnp.zeros_like(acc)
        squares[...] = jnp.zeros_like(squares)
        fresh[...] = jnp.zeros_like(fresh)
        row_reply[...] = jnp.zeros_like(row_reply)

    blank()
    table_all = pltpu.make_async_remote_copy(
        src_ref=landed,
        dst_ref=landed,
        send_sem=table_send,
        recv_sem=table_recv,
        device_id=(mate, me),
        device_id_type=MESH,
    )
    table_all.wait_recv()
    every = jnp.concatenate([landed[number] for number in range(others)] + [tables[...]], 0)
    wide_lane = lax.broadcasted_iota(I32, (groups, 128), 1)

    def before(marks):
        total = marks
        for shift in (1, 2, 4, 8, 16, 32):
            total = total + jnp.where(wide_lane >= shift, pltpu.roll(total, shift, 1), 0)
        return total - marks

    def across_lanes(value):
        for shift in (64, 32, 16, 8, 4, 2, 1):
            value = value + pltpu.roll(value, shift, 1)
        return value

    hits = jnp.where((every == group) & (wide_lane < migrations), 1, 0)
    ranks = before(hits)
    asked = pltpu.roll(every, migrations, 1)
    wanted = jnp.zeros((groups, 128), I32)
    for slot in range(CAP):
        chosen = across_lanes(jnp.where((hits == 1) & (ranks == slot), asked, 0))
        wanted = jnp.where(wide_lane == slot, chosen, wanted)
    mine = jnp.broadcast_to(tables[...], (groups, 128))
    source = lax.broadcasted_iota(I32, (groups, 128), 0)
    marks = jnp.where((source == mine) & (wide_lane < migrations), 1, 0)
    spot = marks * before(marks)
    for shift in (16, 8, 4, 2, 1):
        spot = spot + pltpu.roll(spot, shift, 0)
    spot = ((mine - group + groups) % groups - 1) * CAP + spot
    spot = jnp.minimum(jnp.maximum(spot, 0), others * CAP - 1)
    wish[0:groups, :] = wanted
    wish[groups : groups + 8, :] = jnp.where(wide_lane < migrations, spot, 0)[0:8]
    move = pltpu.make_async_copy(wish, wish_smem, local_sem.at[5])
    move.start()
    move.wait()
    loads[1].wait()

    def page_copy(number):
        return pltpu.make_async_remote_copy(
            src_ref=packed.at[pl.ds(number * CAP, CAP)],
            dst_ref=arrived.at[pl.ds(number * CAP, CAP)],
            send_sem=page_send,
            recv_sem=page_recv,
            device_id=((group + groups - 1 - number) % groups, me),
            device_id_type=MESH,
        )

    def pack(number, carry):
        for slot in range(CAP):
            packed[number * CAP + slot] = pages[wish_smem[number, slot]]
        page_copy(number).start()
        return carry

    lax.fori_loop(0, others, pack, 0)

    for copy in small[2:]:
        copy.wait()
    blocks = gain_rows.shape[0]
    columns = jnp.transpose(jnp.concatenate([gain_rows[...], jnp.zeros((128 - blocks, 128), F32)], 0))
    for block in range(blocks):
        gain[block * 128 : block * 128 + 128, :] = jnp.broadcast_to(columns[:, block : block + 1], (128, 128))

    def consume(owner, part):
        first = owner * width + part * piece
        total = squares[...]
        for strip in range(piece // 16):
            raw = xbuf[owner, pl.ds(part * piece + strip * 16, 16), :].astype(F32)
            factor = gain[pl.ds(first + strip * 16, 16), :]
            scaled = raw * jnp.concatenate([factor] * (tokens // 128), 1)
            xs[strip * 16 : strip * 16 + 16, :] = scaled.astype(BF16)
            square = raw * raw
            total = total + (square[0:8] + square[8:16])
        squares[...] = total
        block = weights[pl.ds(pl.multiple_of(first, 16), piece), :]
        for m in range(tokens // 256):
            at = slice(m * 256, m * 256 + 256)
            acc[at, :] = acc[at, :] + tn(xs[:, at], block)

    def turn_of(i, low, low_parts, high, high_parts):
        half = len(low_parts)
        step = i % (2 * half)
        is_low = step % 2 == 0
        owner = jnp.where(is_low, low, high)
        at_low = low_parts[0] + (step // 2) * (low_parts[1] - low_parts[0])
        at_high = high_parts[0] + (step // 2) * (high_parts[1] - high_parts[0])
        part = jnp.where(is_low, at_low, at_high)
        return jnp.where(i < 2 * half, owner, owner + 1 - 2 * (owner % 2)), part

    for load in (loads[0], loads[2], loads[3], loads[4]):
        load.wait()

    def take_own(i, carry):
        consume(me, i)
        return carry

    def take_sibling(i, carry):
        arrive(sibling, i)
        consume(sibling, i)
        return carry

    lax.fori_loop(0, PARTS, take_own, 0)
    lax.fori_loop(0, PARTS, take_sibling, 0)

    def take(low, low_parts, high, high_parts):
        half = len(low_parts)

        def direct(i, carry):
            consume(*turn_of(i, low, low_parts, high, high_parts))
            return carry

        def indirect(i, carry):
            owner, part = turn_of(i, low, low_parts, high, high_parts)
            arrive(owner, part)
            consume(owner, part)
            return carry

        lax.fori_loop(0, 2 * half, direct, 0)
        lax.fori_loop(2 * half, 4 * half, indirect, 0)

    ahead, behind = tuple(range(PARTS // 2)), tuple(range(PARTS // 2, PARTS))
    for number in range(PARTS // 2):
        arrive(left, ahead[number])
        send(held(left, ahead[number]), left, ahead[number], right)
        arrive(right, behind[-1 - number])
        send(held(right, behind[-1 - number]), right, behind[-1 - number], left)
    for number in range(PARTS // 2):
        send(held(left, ahead[number]), left, ahead[number], sibling)
        send(held(right, behind[-1 - number]), right, behind[-1 - number], sibling)

    node_row = lax.broadcasted_iota(I32, (tree, tree), 0)
    node_col = lax.broadcasted_iota(I32, (tree, tree), 1)
    eye = jnp.where(node_row == node_col, 1.0, 0.0).astype(BF16)
    levels = lax.broadcasted_iota(I32, (8, tree), 0).astype(F32)
    lane = lax.broadcasted_iota(I32, (1, 128), 1)
    angle = jnp.exp((lane % 64).astype(F32) * (-THETA_LOG * 2.0 / 128.0))
    turn = jnp.where(lane < 64, -1.0, 1.0)
    side = jnp.zeros((tree, 128 - tree), F32)

    def grow(number, carry):
        for half in range(2):
            r = number * 2 + half
            up = jnp.where(node_row == parents[pl.ds(r, 1), :], 1.0, 0.0).astype(BF16) + eye
            for _ in range(2):
                up = jnp.minimum(nn(up, up), 1.0).astype(BF16)
            reached = nt(eye, up)
            masks[r] = jnp.concatenate([reached, side], 1)
            depth_row = jnp.sum(up.astype(F32), 0, keepdims=True) - 1.0
            chosen = jnp.where(node_row == jnp.full((tree, tree), leaf[r], I32), reached, 0.0)
            lineage = jnp.sum(chosen, 0, keepdims=True)
            pickers[r] = jnp.where(depth_row == levels, lineage, 0.0)
            depth = jnp.sum(reached, -1, keepdims=True) - 1.0
            base = jnp.full((1, 128), lens[r], I32)
            for j in range(2):
                base = base + jnp.where(jnp.full((1, 128), pair[0, j], I32) == r, far_len[j, group], 0)
            phase = (base.astype(F32) + depth) * angle
            rows = pl.ds(pl.multiple_of(r * tree, tree), tree)
            cosine[rows, :] = jnp.cos(phase)
            sine[rows, :] = jnp.sin(phase) * turn
        return carry

    take(left, ahead, right, behind[::-1])
    lax.fori_loop(0, requests // 2, grow, 0)
    for number in range(PARTS // 2):
        arrive(left, behind[number])
        send(held(left, behind[number]), left, behind[number], sibling)
        arrive(right, ahead[-1 - number])
        send(held(right, ahead[-1 - number]), right, ahead[-1 - number], sibling)
    take(left, behind, right, ahead[::-1])

    page_all = pltpu.make_async_remote_copy(
        src_ref=packed,
        dst_ref=arrived,
        send_sem=page_send,
        recv_sem=page_recv,
        device_id=(mate, me),
        device_id_type=MESH,
    )
    page_all.wait_recv()
    for number in range(migrations):
        pages[pool + number] = arrived[wish_smem[groups, number]]

    for number in range(PARTS // 2):
        arrive(across, ahead[number])
        send(held(across, ahead[number]), across, ahead[number], sibling)
        arrive(across, behind[-1 - number])
        send(held(across, behind[-1 - number]), across, behind[-1 - number], sibling)
    take(across, ahead, across, behind[::-1])

    mean = lax.dot_general(
        squares[...], jnp.full((8, 128), 1.0 / (share * width), F32), (((0,), (0,)), ((), ())),
        precision=lax.Precision.HIGHEST, preferred_element_type=F32,
    )
    scale = lax.rsqrt(mean + 1e-06)
    cosine[...] = cosine[...] * scale
    sine[...] = sine[...] * scale
    fresh[0:tokens, 128:256] = (acc[:, 384:512] * scale).astype(BF16)

    def turned(rows, at):
        value = acc[rows, at : at + 128]
        return (value * cosine[rows, :] + pltpu.roll(value, 64, 1) * sine[rows, :]).astype(BF16)

    def finish(number, carry):
        for half in range(2):
            r = number * 2 + half
            rows = pl.ds(pl.multiple_of(r * tree, tree), tree)
            fresh[rows, 0:128] = turned(rows, 256)
            queries[r, 0:tree, :] = turned(rows, 0)
            queries[r, tree : 2 * tree, :] = turned(rows, 128)
        return carry

    lax.fori_loop(0, requests // 2, finish, 0)
    for j in range(2):
        far_query[j] = queries[pair[0, j]]

    def far_copy(source, target, number):
        return pltpu.make_async_remote_copy(
            src_ref=source,
            dst_ref=target,
            send_sem=far_send.at[number],
            recv_sem=far_recv.at[number],
            device_id=(mate, me),
            device_id_type=MESH,
        )

    ask = far_copy(far_query, far_ask, 0)
    ask.start()

    span = ITEM_PAGES * size
    where = lax.broadcasted_iota(I32, (1, span), 1)
    items = table.shape[1] // ITEM_PAGES

    def score(query, book, row, item, at):
        both = [pages[book[row, item * ITEM_PAGES + k]] for k in range(ITEM_PAGES)]
        for k in range(ITEM_PAGES):
            values[at, k * size : k * size + size, :] = both[k][:, 128:256]
        scores[at] = nt(query, jnp.concatenate([part[:, 0:128] for part in both], 0))

    def gather_up(total, summed, valid, at):
        for part in range(span // 256):
            pieces = []
            for first in (part * 256, part * 256 + 128):
                weight = weigh(scores[at, :, first : first + 128])
                weight = jnp.where(where[:, first : first + 128] < valid, weight, 0.0)
                summed = summed + weight
                pieces.append(weight.astype(BF16))
            total = total + nn(jnp.concatenate(pieces, 1), values[at, part * 256 : part * 256 + 256, :])
        return total, summed

    def run(source, book, length_of, first, last, own, extra=None):
        def body(r, carry):
            query = source[r]
            following = jnp.minimum(r + 1, last - 1)
            length = length_of(r)
            if own:
                new = fresh[pl.ds(pl.multiple_of(r * tree, tree), 128), :]
                mask = masks[r]
                weight = weigh(nt(query, new[:, 0:128])) * jnp.concatenate([mask, mask], 0)
                summed = weight
                total = nn(weight.astype(BF16), new[:, 128:256])
                path[r] = nn(pickers[r].astype(BF16), new[0:tree]).astype(BF16)
            else:
                summed = jnp.zeros((2 * tree, 128), F32)
                total = jnp.zeros((2 * tree, 128), F32)
            for item in range(items):
                if item + 1 < items:
                    score(query, book, r, item + 1, (item + 1) % 2)
                else:
                    score(source[following], book, following, 0, (item + 1) % 2)
                total, summed = gather_up(total, summed, length - item * span, item % 2)
            if own:
                mixed[r] = total
                sums[r] = summed
            else:
                far_reply[r] = total.astype(BF16)
                sums[requests + r] = summed
            if extra is not None:
                extra(r)
            return carry

        score(source[first], book, first, 0, 0)
        lax.fori_loop(first, last, body, 0)

    own_row = lax.broadcasted_iota(I32, (2 * tree, 128), 0)
    own_lane = lax.broadcasted_iota(I32, (2 * tree, 128), 1)

    def settle(r):
        total = mixed[r]
        summed = jnp.sum(sums[r], -1, keepdims=True)
        for j in range(2):
            this = jnp.full((1, 128), pair[0, j], I32) == r
            total = total + jnp.where(this, far_back[j].astype(F32), 0.0)
            spread = jnp.where((own_row == own_lane) & this, row_back[j : j + 1, :], 0.0)
            summed = summed + jnp.sum(spread, -1, keepdims=True)
        final = (total / summed).astype(BF16)
        rows = pl.ds(pl.multiple_of(r * tree, tree), tree)
        out[rows, 0:128] = final[0:tree]
        out[rows, 128:256] = final[tree : 2 * tree]

    run(queries, table, lambda r: lens[r], 0, EARLY, True)
    ask.wait_recv()
    run(far_ask, far_table, lambda r: far_len[r, mate], 0, 2, False)
    for j in range(2):
        summed = jnp.sum(sums[requests + j], -1, keepdims=True)
        row_reply[j : j + 1, :] = jnp.sum(jnp.where(own_row == own_lane, summed, 0.0), 0, keepdims=True)
    replies = far_copy(far_reply, far_back, 1), far_copy(row_reply, row_back, 2)
    for copy in replies:
        copy.start()
    late = 4
    run(queries, table, lambda r: lens[r], EARLY, requests - late, True)
    for copy in replies:
        copy.wait_recv()
    older = (requests - late) // late

    def catch_up(r):
        for number in range(older):
            settle((r - (requests - late)) * older + number)

    run(queries, table, lambda r: lens[r], requests - late, requests, True, catch_up)
    for number in range(late):
        settle(requests - late + number)

    ask.wait_send()
    for copy in replies:
        copy.wait_send()
    for copy in sent:
        copy.wait_send()
    page_all.wait_send()
    table_all.wait_send()


def body(
    mesh, hidden, norm_gain, q_weight, k_weight, v_weight, kv_pages, page_table, cache_len, tree_parent,
    accept_node, pair_slot, far_len, far_table, mig_src, mig_page,
):
    requests, tree = tree_parent.shape
    pool, page_size, _, entry = kv_pages.shape
    page = (page_size, entry)
    tokens, width = hidden.shape
    groups, share = mesh.shape["grp"], mesh.shape["tp"]
    migrations = mig_src.shape[0]
    others = groups - 1
    blocks = norm_gain.shape[0] // 128
    span = ITEM_PAGES * page_size
    rows = 2 * tree
    dma = pltpu.SemaphoreType.DMA
    vmem, smem = pltpu.VMEM, pltpu.SMEM
    out, path = pl.pallas_call(
        functools.partial(kernel, groups, share),
        out_shape=(
            jax.ShapeDtypeStruct((tokens, 256), BF16),
            jax.ShapeDtypeStruct((requests, 8, 256), BF16),
        ),
        in_specs=[pl.BlockSpec(memory_space=pl.ANY)] * 15,
        out_specs=(pl.BlockSpec(memory_space=pltpu.VMEM),) * 2,
        scratch_shapes=[
            smem(page_table.shape, I32),
            smem(cache_len.shape, I32),
            smem(pair_slot.shape, I32),
            smem(accept_node.shape, I32),
            smem(far_len.shape[::-1], I32),
            smem(far_table.shape, I32),
            vmem((1, migrations), I32),
            vmem((1, migrations), I32),
            vmem((blocks, 128), F32),
            vmem(tree_parent.shape, I32),
            vmem((1, 2 * migrations), I32),
            vmem((others, 1, 2 * migrations), I32),
            vmem((groups + 8, 128), I32),
            smem((groups + 8, 128), I32),
            vmem((share * width, 128), F32),
            vmem((share, width, tokens), BF16),
            vmem((share * width, 512), BF16),
            vmem((tokens, 512), F32),
            vmem((8, tokens), F32),
            vmem((width // PARTS, tokens), BF16),
            vmem((tokens, 128), F32),
            vmem((tokens, 128), F32),
            vmem((pool + migrations,) + page, BF16),
            vmem((others * CAP,) + page, BF16),
            vmem((others * CAP,) + page, BF16),
            vmem((requests, tree, 128), F32),
            vmem((requests, 8, tree), F32),
            vmem((requests, rows, 128), BF16),
            vmem((tokens + 128 - tree, 256), BF16),
            vmem((2, rows, span), F32),
            vmem((2, span, 128), BF16),
            vmem((requests, rows, 128), F32),
            vmem((requests + 2, rows, 128), F32),
            vmem((2, rows, 128), BF16),
            vmem((2, rows, 128), BF16),
            vmem((2, rows, 128), BF16),
            vmem((2, rows, 128), BF16),
            vmem((8, 128), F32),
            vmem((8, 128), F32),
            dma((10,)),
            dma((6,)),
            dma((3 * PARTS + 4 * PARTS,)),
            dma((share, PARTS)),
            dma,
            dma,
            dma,
            dma,
            dma((3,)),
            dma((3,)),
        ],
        compiler_params=pltpu.CompilerParams(
            collective_id=0, has_side_effects=True, vmem_limit_bytes=56 << 20
        ),
        name="tree_attention",
    )(
        page_table, cache_len, pair_slot, accept_node, far_len.T, far_table, mig_src[None, :], mig_page[None, :],
        norm_gain.reshape(blocks, 128), tree_parent, hidden.T, kv_pages.reshape((pool,) + page), q_weight,
        k_weight, v_weight,
    )
    return out, path[:, :ACCEPT].reshape(requests * ACCEPT, 1, entry)


def solution(mesh):
    in_specs = (
        P("grp", "tp"),
        P(),
        P(None, "tp"),
        P(None, "tp"),
        P(None, "tp"),
        P("grp", None, "tp", None),
        P("grp", None),
        P("grp"),
        P("grp", None),
        P("grp"),
        P("grp", None),
        P(),
        P("grp", None),
        P("grp"),
        P("grp"),
    )
    out_specs = (P("grp", "tp"), P("grp", "tp", None))
    return jax.shard_map(
        functools.partial(body, mesh), mesh=mesh, in_specs=in_specs, out_specs=out_specs, check_vma=False
    )
```

time: 162 us -> 72.6 us (0.45)
  the two profiles are of different devices: /device:TPU:120 before, /device:TPU:1 now
where the time goes in v2:
time: 72.6 us; the launch traced here: 72.4 us
  Pallas kernels  68.5 us (94%)
  local copies, waits for them, and re-layouts  3.25 us (4%)
    pallas_call x1, Pallas kernels, body(): pl.pallas_call(functools.partial(kernel, groups, share), out_shape=(jax.S...  68.5 us
    unnamed x1, local copies, waits for them, and re-layouts  1.77 us
    reshape x1, local copies, waits for them, and re-layouts, body(): return (out, path[:, :ACCEPT].reshape(requests * ACCEPT, 1, entry))  1.48 us

profile of v2, /device:TPU:1, one launch (start us, length us, event | category | flops | bytes accessed | tf_op | source)
XLA Modules:
  0.0 72.4 jit_solution(12329924106321294363)
XLA Ops:
  0.6 68.5 %tree_attention.1 = (bf16[768,256]{1,0:T(8,128)(2,1)}, bf16[16,8,256]{2,1,0:T(8,128)(2,1)}) custom-call(s32[16,256]{1,0:T(8,128)} %table_hbm.1, s32[16]{0:T(128)} %lens_hbm.1, s32[1,2]{1,0:T(1,128)} %pair_hbm.1, s32[16]{0:T(128)} %leaf_hbm.1, s32[2,32]{1,0:T(2,128)} %bitcast.11, s32[2,256]{1,0:T(2,128)} %far_table_hbm.1, s32[1,64]{1,0:T(1,128)} %bitcast.12, ...), custom_call_target="tpu_custom_call" | custom-call | tf_op jit(solution)/shard_map/tree_attention/pallas_call | solution.py:526
  69.1 1.5 %reshape.15 = bf16[80,1,256]{2,0,1:T(8,128)(2,1)} reshape(bf16[16,5,256]{2,1,0:T(8,128)(2,1)} %bitcast.9) | data formatting | bytes 81920 | tf_op jit(solution)/shard_map/reshape | solution.py:594
  70.6 1.8 %copy.18 = bf16[768,256]{1,0:T(8,128)(2,1)} copy(bf16[768,256]{1,0:T(8,128)(2,1)} %get-tuple-element.8) | data formatting | bytes 786432

commit v3 on v2

--- a/solution.py
+++ b/solution.py
@@ -45,8 +45,8 @@
     table, lens, pair, leaf, far_len, far_table, own_src, own_page, gain_rows, parents,
     tables, landed, wish, wish_smem, gain, xbuf, weights, acc, squares, xs, cosine, sine, pages, packed, arrived,
     masks, pickers, queries, fresh, scores, values, mixed, sums, far_query, far_ask, far_reply, far_back, row_reply,
-    row_back,
-    small_sem, local_sem, send_sem, recv_sem, table_send, table_recv, page_send, page_recv, far_send, far_recv,
+    row_back, chain,
+    small_sem, local_sem, send_sem, recv_sem, table_send, table_recv, page_send, page_recv, far_send, far_recv, passed,
 ):
     group = lax.axis_index("grp")
     me = lax.axis_index("tp")
@@ -88,24 +88,32 @@
         pltpu.make_async_copy(k_hbm, weights.at[:, pl.ds(256, 128)], local_sem.at[3]),
         pltpu.make_async_copy(v_hbm, weights.at[:, pl.ds(384, 128)], local_sem.at[4]),
     ]
-    small[0].start()
-    small[1].start()
+    for copy in small[0:2] + loads[1:2] + loads[0:1] + loads[2:] + small[2:]:
+        copy.start()
 
     barrier = pltpu.get_barrier_semaphore()
-    for peer in (left, right, sibling):
-        pl.semaphore_signal(barrier, inc=1, device_id=(group, peer), device_id_type=MESH)
+    for peer in (left // 2, right // 2):
+        pl.semaphore_signal(barrier, inc=1, device_id=(group, peer * 2), device_id_type=MESH)
+
+    @pl.when(core == 1)
+    def _():
+        pl.semaphore_signal(barrier, inc=1, device_id=(group, sibling), device_id_type=MESH)
 
     def greet(number, carry):
         peer = (group + 1 + number) % groups
-        pl.semaphore_signal(barrier, inc=1, device_id=(peer, me), device_id_type=MESH)
+        pl.semaphore_signal(barrier, inc=1, device_id=(peer, chip * 2 + 1), device_id_type=MESH)
         return carry
 
     lax.fori_loop(0, others, greet, 0)
-    small[0].wait()
-    small[1].wait()
-    tables[:, 0:migrations] = own_src[...]
-    tables[:, migrations : 2 * migrations] = own_page[...]
-    pl.semaphore_wait(barrier, 3 + others)
+
+    @pl.when(core == 0)
+    def _():
+        pl.semaphore_wait(barrier, 5)
+        pl.semaphore_signal(passed, inc=1, device_id=(group, sibling), device_id_type=MESH)
+
+    @pl.when(core == 1)
+    def _():
+        pl.semaphore_wait(passed, 1)
 
     sent = []
 
@@ -154,21 +162,31 @@
     for part in range(PARTS):
         send(own_part(part), me, part, right)
         send(own_part(PARTS - 1 - part), me, PARTS - 1 - part, left)
-        if part == 0:
-            lax.fori_loop(0, others, tell, 0)
     for part in range(PARTS):
         send(own_part(part), me, part, sibling)
-    for copy in loads + small[2:]:
-        copy.start()
+    small[0].wait()
+    small[1].wait()
+    tables[:, 0:migrations] = own_src[...]
+    tables[:, migrations : 2 * migrations] = own_page[...]
 
     def blank():
-        pages[pl.ds(pool, migrations)] = jnp.zeros((migrations,) + pages.shape[1:], BF16)
         acc[...] = jnp.zeros_like(acc)
         squares[...] = jnp.zeros_like(squares)
         fresh[...] = jnp.zeros_like(fresh)
         row_reply[...] = jnp.zeros_like(row_reply)
 
-    blank()
+    pages[pl.ds(pool, migrations)] = jnp.zeros((migrations,) + pages.shape[1:], BF16)
+
+    @pl.when(core == 1)
+    def _():
+        pl.semaphore_wait(barrier, 2 * others)
+        pl.semaphore_signal(passed, inc=1, device_id=(group, sibling), device_id_type=MESH)
+
+    @pl.when(core == 0)
+    def _():
+        pl.semaphore_wait(passed, 1)
+
+    lax.fori_loop(0, others, tell, 0)
     table_all = pltpu.make_async_remote_copy(
         src_ref=landed,
         dst_ref=landed,
@@ -224,13 +242,11 @@
             device_id_type=MESH,
         )
 
-    def pack(number, carry):
+    for number in range(others):
         for slot in range(CAP):
             packed[number * CAP + slot] = pages[wish_smem[number, slot]]
         page_copy(number).start()
-        return carry
-
-    lax.fori_loop(0, others, pack, 0)
+    blank()
 
     for copy in small[2:]:
         copy.wait()
@@ -436,7 +452,7 @@
                 weight = weigh(nt(query, new[:, 0:128])) * jnp.concatenate([mask, mask], 0)
                 summed = weight
                 total = nn(weight.astype(BF16), new[:, 128:256])
-                path[r] = nn(pickers[r].astype(BF16), new[0:tree]).astype(BF16)
+                chain[pl.ds(pl.multiple_of(r * 8, 8), 8), :] = nn(pickers[r].astype(BF16), new[0:tree])
             else:
                 summed = jnp.zeros((2 * tree, 128), F32)
                 total = jnp.zeros((2 * tree, 128), F32)
@@ -495,6 +511,10 @@
             settle((r - (requests - late)) * older + number)
 
     run(queries, table, lambda r: lens[r], requests - late, requests, True, catch_up)
+    row_of = lax.broadcasted_iota(I32, path.shape[0:1] + (8 * requests,), 0)
+    place = lax.broadcasted_iota(I32, path.shape[0:1] + (8 * requests,), 1)
+    compact = jnp.where(place == row_of // ACCEPT * 8 + row_of % ACCEPT, 1.0, 0.0).astype(BF16)
+    path[...] = nn(compact, chain[...].astype(BF16)).astype(BF16)
     for number in range(late):
         settle(requests - late + number)
 
@@ -505,6 +525,17 @@
         copy.wait_send()
     page_all.wait_send()
     table_all.wait_send()
+
+
+def deliver(out, path, out_final, path_final, sems):
+    copies = (
+        pltpu.make_async_copy(out, out_final, sems.at[0]),
+        pltpu.make_async_copy(path, path_final, sems.at[1]),
+    )
+    for copy in copies:
+        copy.start()
+    for copy in copies:
+        copy.wait()
 
 
 def body(
@@ -527,7 +558,7 @@
         functools.partial(kernel, groups, share),
         out_shape=(
             jax.ShapeDtypeStruct((tokens, 256), BF16),
-            jax.ShapeDtypeStruct((requests, 8, 256), BF16),
+            jax.ShapeDtypeStruct((requests * ACCEPT, 256), BF16),
         ),
         in_specs=[pl.BlockSpec(memory_space=pl.ANY)] * 15,
         out_specs=(pl.BlockSpec(memory_space=pltpu.VMEM),) * 2,
@@ -571,6 +602,7 @@
             vmem((2, rows, 128), BF16),
             vmem((8, 128), F32),
             vmem((8, 128), F32),
+            vmem((8 * requests, 256), F32),
             dma((10,)),
             dma((6,)),
             dma((3 * PARTS + 4 * PARTS,)),
@@ -581,6 +613,7 @@
             dma,
             dma((3,)),
             dma((3,)),
+            pltpu.SemaphoreType.REGULAR,
         ],
         compiler_params=pltpu.CompilerParams(
             collective_id=0, has_side_effects=True, vmem_limit_bytes=56 << 20
@@ -591,7 +624,18 @@
         norm_gain.reshape(blocks, 128), tree_parent, hidden.T, kv_pages.reshape((pool,) + page), q_weight,
         k_weight, v_weight,
     )
-    return out, path[:, :ACCEPT].reshape(requests * ACCEPT, 1, entry)
+    out, path = pl.pallas_call(
+        deliver,
+        out_shape=(
+            jax.ShapeDtypeStruct(out.shape, BF16),
+            jax.ShapeDtypeStruct(path.shape, BF16),
+        ),
+        in_specs=[pl.BlockSpec(memory_space=pltpu.VMEM)] * 2,
+        out_specs=(pl.BlockSpec(memory_space=pl.ANY),) * 2,
+        scratch_shapes=[dma((2,))],
+        name="deliver",
+    )(out, path)
+    return out, path[:, None, :]
 
 
 def solution(mesh):

time: 72.6 us -> 71.5 us (0.985)
  local copies, waits for them, and re-layouts: 3.25 us -> 0 us
  Pallas kernels: 68.5 us -> 70.7 us
    unnamed x1 -> x0, local copies, waits for them, and re-layouts: 1.77 us -> none
    pallas_call x0 -> x1, Pallas kernels: none -> 1.76 us  [body(): pl.pallas_call(deliver, out_shape=(jax.ShapeDtypeStruct(out.shape, BF16),...]
    reshape x1 -> x0, local copies, waits for them, and re-layouts: 1.48 us -> none  [body(): return (out, path[:, :ACCEPT].reshape(requests * ACCEPT, 1, entry))]
where the time goes in v3:
time: 71.5 us; the launch traced here: 71.4 us
  Pallas kernels  70.7 us (99%)
    pallas_call x1, Pallas kernels, body(): pl.pallas_call(functools.partial(kernel, groups, share), out_shape=(jax.S...  69 us
    pallas_call x1, Pallas kernels, body(): pl.pallas_call(deliver, out_shape=(jax.ShapeDtypeStruct(out.shape, BF16),...  1.76 us

profile of v3, /device:TPU:1, one launch (start us, length us, event | category | flops | bytes accessed | tf_op | source)
XLA Modules:
  0.0 71.4 jit_solution(13984583570104213706)
XLA Ops:
  0.6 69.0 %tree_attention.1 = (bf16[768,256]{1,0:T(8,128)(2,1)}, bf16[80,256]{1,0:T(8,128)(2,1)}) custom-call(s32[16,256]{1,0:T(8,128)} %table_hbm.1, s32[16]{0:T(128)} %lens_hbm.1, s32[1,2]{1,0:T(1,128)} %pair_hbm.1, s32[16]{0:T(128)} %leaf_hbm.1, s32[2,32]{1,0:T(2,128)} %bitcast.10, s32[2,256]{1,0:T(2,128)} %far_table_hbm.1, s32[1,64]{1,0:T(1,128)} %bitcast.11, ...), custom_call_target="tpu_custom_call" | custom-call | tf_op jit(solution)/shard_map/tree_attention/pallas_call | solution.py:557
  69.6 1.8 %deliver.1 = (bf16[768,256]{1,0:T(8,128)(2,1)}, bf16[80,256]{1,0:T(8,128)(2,1)}) custom-call(bf16[768,256]{1,0:T(8,128)(2,1)} %get-tuple-element.6.out, bf16[80,256]{1,0:T(8,128)(2,1)} %get-tuple-element.7.path), custom_call_target="tpu_custom_call" | custom-call | tf_op jit(solution)/shard_map/deliver/pallas_call | solution.py:627

commit v4 on v3

--- a/solution.py
+++ b/solution.py
@@ -99,12 +99,20 @@
     def _():
         pl.semaphore_signal(barrier, inc=1, device_id=(group, sibling), device_id_type=MESH)
 
-    def greet(number, carry):
-        peer = (group + 1 + number) % groups
-        pl.semaphore_signal(barrier, inc=1, device_id=(peer, chip * 2 + 1), device_id_type=MESH)
-        return carry
-
-    lax.fori_loop(0, others, greet, 0)
+    def ahead_of(number):
+        peer = group + 1 + number
+        return jnp.where(peer >= groups, peer - groups, peer)
+
+    def behind_of(number):
+        peer = group - 1 - number
+        return jnp.where(peer < 0, peer + groups, peer)
+
+    def greet():
+        for number in range(others):
+            peer = (ahead_of(number), chip * 2 + 1)
+            pl.semaphore_signal(barrier, inc=1, device_id=peer, device_id_type=MESH)
+
+    greet()
 
     @pl.when(core == 0)
     def _():
@@ -151,13 +159,9 @@
             dst_ref=landed.at[number],
             send_sem=table_send,
             recv_sem=table_recv,
-            device_id=((group + 1 + number) % groups, me),
+            device_id=(ahead_of(number), me),
             device_id_type=MESH,
         )
-
-    def tell(number, carry):
-        table_copy(number).start()
-        return carry
 
     for part in range(PARTS):
         send(own_part(part), me, part, right)
@@ -186,7 +190,8 @@
     def _():
         pl.semaphore_wait(passed, 1)
 
-    lax.fori_loop(0, others, tell, 0)
+    for number in range(others):
+        table_copy(number).start()
     table_all = pltpu.make_async_remote_copy(
         src_ref=landed,
         dst_ref=landed,
@@ -238,7 +243,7 @@
             dst_ref=arrived.at[pl.ds(number * CAP, CAP)],
             send_sem=page_send,
             recv_sem=page_recv,
-            device_id=((group + groups - 1 - number) % groups, me),
+            device_id=(behind_of(number), me),
             device_id_type=MESH,
         )
 
@@ -370,9 +375,6 @@
         device_id=(mate, me),
         device_id_type=MESH,
     )
-    page_all.wait_recv()
-    for number in range(migrations):
-        pages[pool + number] = arrived[wish_smem[groups, number]]
 
     for number in range(PARTS // 2):
         arrive(across, ahead[number])
@@ -419,6 +421,9 @@
 
     ask = far_copy(far_query, far_ask, 0)
     ask.start()
+    page_all.wait_recv()
+    for number in range(migrations):
+        pages[pool + number] = arrived[wish_smem[groups, number]]
 
     span = ITEM_PAGES * size
     where = lax.broadcasted_iota(I32, (1, span), 1)

time: 71.5 us -> 65.8 us (0.920)
  Pallas kernels: 70.7 us -> 64.9 us
    pallas_call x1, Pallas kernels: 69 us -> 63.2 us  [body(): pl.pallas_call(functools.partial(kernel, groups, share), out_shape=(jax.S...]
where the time goes in v4:
time: 65.8 us; the launch traced here: 65.6 us
  Pallas kernels  64.9 us (99%)
    pallas_call x1, Pallas kernels, body(): pl.pallas_call(functools.partial(kernel, groups, share), out_shape=(jax.S...  63.2 us
    pallas_call x1, Pallas kernels, body(): pl.pallas_call(deliver, out_shape=(jax.ShapeDtypeStruct(out.shape, BF16),...  1.76 us

profile of v4, /device:TPU:1, one launch (start us, length us, event | category | flops | bytes accessed | tf_op | source)
XLA Modules:
  0.0 65.6 jit_solution(4870723040992054513)
XLA Ops:
  0.6 63.2 %tree_attention.1 = (bf16[768,256]{1,0:T(8,128)(2,1)}, bf16[80,256]{1,0:T(8,128)(2,1)}) custom-call(s32[16,256]{1,0:T(8,128)} %table_hbm.1, s32[16]{0:T(128)} %lens_hbm.1, s32[1,2]{1,0:T(1,128)} %pair_hbm.1, s32[16]{0:T(128)} %leaf_hbm.1, s32[2,32]{1,0:T(2,128)} %bitcast.10, s32[2,256]{1,0:T(2,128)} %far_table_hbm.1, s32[1,64]{1,0:T(1,128)} %bitcast.11, ...), custom_call_target="tpu_custom_call" | custom-call | tf_op jit(solution)/shard_map/tree_attention/pallas_call | solution.py:562
  63.8 1.8 %deliver.1 = (bf16[768,256]{1,0:T(8,128)(2,1)}, bf16[80,256]{1,0:T(8,128)(2,1)}) custom-call(bf16[768,256]{1,0:T(8,128)(2,1)} %get-tuple-element.6.out, bf16[80,256]{1,0:T(8,128)(2,1)} %get-tuple-element.7.path), custom_call_target="tpu_custom_call" | custom-call | tf_op jit(solution)/shard_map/deliver/pallas_call | solution.py:632

commit v5 on v4

--- a/solution.py
+++ b/solution.py
@@ -247,7 +247,7 @@
             device_id_type=MESH,
         )
 
-    for number in range(others):
+    for number in sorted(range(others), key=lambda step: abs(2 * step - others + 1)):
         for slot in range(CAP):
             packed[number * CAP + slot] = pages[wish_smem[number, slot]]
         page_copy(number).start()

time: 65.8 us -> 65.6 us (level)
  no operation moved by 1% of the time
where the time goes in v5:
time: 65.6 us; the launch traced here: 65.5 us
  Pallas kernels  64.8 us (99%)
    pallas_call x1, Pallas kernels, body(): pl.pallas_call(functools.partial(kernel, groups, share), out_shape=(jax.S...  63.1 us
    pallas_call x1, Pallas kernels, body(): pl.pallas_call(deliver, out_shape=(jax.ShapeDtypeStruct(out.shape, BF16),...  1.76 us

profile of v5, /device:TPU:1, one launch (start us, length us, event | category | flops | bytes accessed | tf_op | source)
XLA Modules:
  0.0 65.5 jit_solution(17834346317497304726)
XLA Ops:
  0.6 63.1 %tree_attention.1 = (bf16[768,256]{1,0:T(8,128)(2,1)}, bf16[80,256]{1,0:T(8,128)(2,1)}) custom-call(s32[16,256]{1,0:T(8,128)} %table_hbm.1, s32[16]{0:T(128)} %lens_hbm.1, s32[1,2]{1,0:T(1,128)} %pair_hbm.1, s32[16]{0:T(128)} %leaf_hbm.1, s32[2,32]{1,0:T(2,128)} %bitcast.10, s32[2,256]{1,0:T(2,128)} %far_table_hbm.1, s32[1,64]{1,0:T(1,128)} %bitcast.11, ...), custom_call_target="tpu_custom_call" | custom-call | tf_op jit(solution)/shard_map/tree_attention/pallas_call | solution.py:562
  63.7 1.8 %deliver.1 = (bf16[768,256]{1,0:T(8,128)(2,1)}, bf16[80,256]{1,0:T(8,128)(2,1)}) custom-call(bf16[768,256]{1,0:T(8,128)(2,1)} %get-tuple-element.6.out, bf16[80,256]{1,0:T(8,128)(2,1)} %get-tuple-element.7.path), custom_call_target="tpu_custom_call" | custom-call | tf_op jit(solution)/shard_map/deliver/pallas_call | solution.py:632
